TPU v7x, 32 devices: a whole 2x2x4 slice. The times are simulated.
32 devices in a mesh: row: 8 (over y, x, core), feat: 4 (over z).
Axes of the slice: x: 2, y: 2, z: 4, core: 2. Of those that a mesh axis runs over, the one named last changes fastest.
Arguments:
- bins: int32 [1024, 65536], P('feat', 'row'), may hold values from 0 to 255
- grads: bfloat16 [65536], P('row'), may hold values from -6 to 6
- hess: bfloat16 [65536], P('row'), may hold values from 0.049804688 to 1
- node: int32 [65536], P('row'), may hold values from 0 to 7
Outputs:
- shortfall: float32 [1024, 8, 256], P(('feat', 'row'))
- best: float32 [8], replicated
All inputs are finite; a program needn't handle non-finite values.
Results may differ from a plain program's by a relative error of at most 0.0003.
Values sent between devices are 32-bit elements; how exact they have to be, the bound alone decides.
A program may use at most 64 MiB of HBM per device.

v0:
```python
import functools
import jax
import jax.numpy as jnp
from jax import lax
from jax.experimental import pallas as pl
from jax.experimental.pallas import tpu as pltpu
from jax.sharding import PartitionSpec as P

BINS = 256
NODES = 8
LANES = 128
SUBLANES = 8
LOW = 64
TILE = 256
GROUP = TILE // LOW
HALVES = LANES // LOW
TOPS = BINS // LANES
SLOTS = NODES * TOPS
LINES = 2 * SLOTS
MESH = pl.DeviceIdType.MESH


def partner(me, k, n):
    if n & (n - 1):
        return (me + k) % n
    out, weight = 0, 1
    while weight < n:
        out = out + (((me // weight) % 2 + (k // weight) % 2) % 2) * weight
        weight *= 2
    return out


def kernel(
    n, m, block, chunks, bins_hbm, node_ref, g_ref, h_ref, out_ref, best_ref,
    bins_buf, high_ref, low_ref, g_all, h_all, acc_ref, stage, landed, row_best, feat_best,
    load_sem, send_sem, recv_sem, row_send, row_recv, feat_send, feat_recv,
):
    rows = bins_buf.shape[2]
    me = lax.axis_index("row")
    mine = lax.axis_index("feat")
    steps = n * chunks
    sent = (n - 1) * chunks

    def place_of(s):
        return (partner(me, n - 1 - s // chunks, n) * chunks + s % chunks) * block

    def load(s):
        start = pl.multiple_of((place_of(s) // SUBLANES) * SUBLANES, SUBLANES)
        return pltpu.make_async_copy(
            bins_hbm.at[pl.ds(start, bins_buf.shape[1]), :], bins_buf.at[s % 2], load_sem.at[s % 2]
        )

    def send(s):
        k = n - 1 - s // chunks
        return pltpu.make_async_remote_copy(
            src_ref=stage.at[s],
            dst_ref=landed.at[s],
            send_sem=send_sem.at[s],
            recv_sem=recv_sem.at[s],
            device_id={"row": partner(me, k, n)},
            device_id_type=MESH,
        )

    load(0).start()
    barrier = pltpu.get_barrier_semaphore()
    for k in range(1, n):
        pl.semaphore_signal(barrier, inc=1, device_id={"row": (me + k) % n}, device_id_type=MESH)
    for k in range(1, m):
        pl.semaphore_signal(barrier, inc=1, device_id={"feat": (mine + k) % m}, device_id_type=MESH)

    g = g_ref[...].astype(jnp.float32)
    h = h_ref[...].astype(jnp.float32)
    for i in range(rows // LANES):
        cols = slice(i * LANES, (i + 1) * LANES)
        g_all[:, cols] = jnp.broadcast_to(g[i : i + 1, :], (SLOTS, LANES)).astype(jnp.bfloat16)
        h_all[:, cols] = jnp.broadcast_to(h[i : i + 1, :], (SLOTS, LANES)).astype(jnp.bfloat16)
    pl.semaphore_wait(barrier, n + m - 2)

    def step(s, carry):
        load(s).wait()

        @pl.when(s + 1 < steps)
        def _():
            load(s + 1).start()

        @pl.when((s >= 1) & (s <= sent))
        def _():
            send(s - 1).start()

        offset = 0 if block % SUBLANES == 0 else place_of(s) % SUBLANES
        bins = bins_buf[s % 2]
        upper = bins >= LANES
        rest = jnp.where(upper, bins - LANES, bins)
        second = rest >= LOW
        slot = node_ref[...] + jnp.where(upper, NODES, 0)
        high_ref[...] = jnp.where(second, slot + SLOTS, slot).astype(jnp.float32)
        low_ref[...] = jnp.where(second, rest - LOW, rest).astype(jnp.float32)
        place = lax.broadcasted_iota(jnp.int32, (SLOTS, rows), 0).astype(jnp.bfloat16)
        zero = jnp.zeros((SLOTS, rows), jnp.bfloat16)
        one = jnp.ones((SLOTS, rows), jnp.bfloat16)
        for first in range(0, block, GROUP):
            left, right = [], []
            for f in range(first, first + GROUP):
                row = pl.ds(offset + f, 1)
                high = jnp.broadcast_to(high_ref[row, :], (SLOTS, rows)).astype(jnp.bfloat16)
                low = jnp.broadcast_to(low_ref[row, :], (SLOTS, rows)).astype(jnp.bfloat16)
                for j in range(HALVES):
                    here = high == place + jnp.asarray(SLOTS * j, jnp.bfloat16)
                    left += [jnp.where(here, g_all[...], zero), jnp.where(here, h_all[...], zero)]
                for j in range(LOW // SLOTS):
                    here = low == place + jnp.asarray(SLOTS * j, jnp.bfloat16)
                    right.append(jnp.where(here, one, zero))
            acc_ref[...] = lax.dot_general(
                jnp.concatenate(left, 0),
                jnp.concatenate(right, 0),
                (((1,), (1,)), ((), ())),
                preferred_element_type=jnp.float32,
            )
            for i in range(GROUP):
                parts = []
                for j in range(HALVES):
                    top = (i * HALVES + j) * LINES
                    parts.append(acc_ref[top : top + LINES, i * LOW : (i + 1) * LOW])
                stage[s, first + i] = jnp.concatenate(parts, 1)
        return carry

    lax.fori_loop(0, steps, step, 0)

    def drain(s, carry):
        send(s).wait()
        return carry

    lax.fori_loop(0, sent, drain, 0)

    lane = lax.broadcasted_iota(jnp.int32, (block * 2 * TOPS * NODES, LANES), 1)

    def finish(c, top_gain):
        def add(k, total):
            return total + landed[k * chunks + c]

        x = lax.fori_loop(0, n - 1, add, stage[sent + c])
        x = x.reshape(block * LINES, LANES)
        shift = 1
        while shift < LANES:
            x = x + jnp.where(lane >= shift, pltpu.roll(x, shift, 1), 0.0)
            shift *= 2
        x = x.reshape(block, 2, TOPS, NODES, LANES)
        left, total = [], jnp.zeros((block, 2, NODES, LANES), jnp.float32)
        for t in range(TOPS):
            left.append(x[:, :, t] + total)
            total = total + jnp.broadcast_to(x[:, :, t, :, LANES - 1 :], total.shape)
        gt, ht = total[:, 0], total[:, 1]
        base = gt * gt / (ht + 1.0)
        for t in range(TOPS):
            gl, hl = left[t][:, 0], left[t][:, 1]
            gain = gl * gl / (hl + 1.0)
            gain = gain + (gt - gl) * (gt - gl) / (ht - hl + 1.0)
            gain = gain - base
            out_ref[pl.ds(c * block, block), :, t * LANES : (t + 1) * LANES] = gain
            top_gain = jnp.maximum(top_gain, jnp.max(gain, axis=0))
        return top_gain

    top_gain = lax.fori_loop(0, chunks, finish, jnp.full((NODES, LANES), -jnp.inf, jnp.float32))

    def exchange(value, slots, count, axis, index, sems, arrived):
        slots[0] = jnp.broadcast_to(jnp.max(value, axis=1, keepdims=True), (NODES, LANES))
        copies = []
        for k in range(1, count):
            copies.append(
                pltpu.make_async_remote_copy(
                    src_ref=slots.at[0],
                    dst_ref=slots.at[k],
                    send_sem=sems.at[k - 1],
                    recv_sem=arrived.at[k - 1],
                    device_id={axis: (index + k) % count},
                    device_id_type=MESH,
                )
            )
            copies[-1].start()
        for copy in copies:
            copy.wait()
        best = slots[0]
        for k in range(1, count):
            best = jnp.maximum(best, slots[k])
        return best

    best = exchange(top_gain, row_best, n, "row", me, row_send, row_recv)
    best = exchange(best, feat_best, m, "feat", mine, feat_send, feat_recv)
    across = lax.broadcasted_iota(jnp.int32, (NODES, LANES), 1)
    down = lax.broadcasted_iota(jnp.int32, (NODES, LANES), 0)
    flat = jnp.max(jnp.where(across == down, best, -jnp.inf), axis=0, keepdims=True)
    best_ref[...] = flat[:, :NODES]


def solution(mesh):
    n, m = mesh.shape["row"], mesh.shape["feat"]

    def per_device(bins, grads, hess, node):
        features, rows = bins.shape
        own = features // n
        block = own if own < SUBLANES else next(b for b in (2 * SUBLANES, SUBLANES) if own % b == 0)
        held = max(block, SUBLANES)
        chunks = own // block
        vmem = pl.BlockSpec(memory_space=pltpu.VMEM)
        piece = (block, LINES, LANES)
        out, best = pl.pallas_call(
            functools.partial(kernel, n, m, block, chunks),
            in_specs=[pl.BlockSpec(memory_space=pl.ANY), vmem, vmem, vmem],
            out_specs=(vmem, vmem),
            out_shape=(
                jax.ShapeDtypeStruct((own, NODES, BINS), jnp.float32),
                jax.ShapeDtypeStruct((1, NODES), jnp.float32),
            ),
            scratch_shapes=[
                pltpu.VMEM((2, held, rows), jnp.int32),
                pltpu.VMEM((held, rows), jnp.float32),
                pltpu.VMEM((held, rows), jnp.float32),
                pltpu.VMEM((SLOTS, rows), jnp.bfloat16),
                pltpu.VMEM((SLOTS, rows), jnp.bfloat16),
                pltpu.VMEM((GROUP * HALVES * LINES, TILE), jnp.float32),
                pltpu.VMEM((n * chunks,) + piece, jnp.float32),
                pltpu.VMEM(((n - 1) * chunks,) + piece, jnp.float32),
                pltpu.VMEM((n, NODES, LANES), jnp.float32),
                pltpu.VMEM((m, NODES, LANES), jnp.float32),
                pltpu.SemaphoreType.DMA((2,)),
                pltpu.SemaphoreType.DMA(((n - 1) * chunks,)),
                pltpu.SemaphoreType.DMA(((n - 1) * chunks,)),
                pltpu.SemaphoreType.DMA((n - 1,)),
                pltpu.SemaphoreType.DMA((n - 1,)),
                pltpu.SemaphoreType.DMA((m - 1,)),
                pltpu.SemaphoreType.DMA((m - 1,)),
            ],
            compiler_params=pltpu.CompilerParams(
                collective_id=0, has_side_effects=True, vmem_limit_bytes=56 << 20
            ),
        )(bins, node.reshape(1, rows), grads.reshape(-1, LANES), hess.reshape(-1, LANES))
        best = best.reshape(NODES)
        return out - best[None, :, None], best

    return jax.shard_map(
        per_device,
        mesh=mesh,
        in_specs=(P("feat", "row"), P("row"), P("row"), P("row")),
        out_specs=(P(("feat", "row"), None, None), P()),
        check_vma=False,
    )
```

profile of v0, /device:TPU:0, one launch (start us, length us, event | category | flops | bytes accessed | tf_op | source)
XLA Modules:
  0.0 94.2 jit_solution(16406904534879633901)
XLA Ops:
  0.6 90.7 %shard_map.59 = (f32[32,8,256]{2,1,0:T(8,128)}, f32[1,8]{1,0:T(1,128)}) custom-call(s32[256,8192]{1,0:T(8,128)} %bins_hbm.1, s32[1,8192]{1,0:T(1,128)} %bitcast.4, bf16[64,128]{1,0:T(8,128)(2,1)} %bitcast.5, bf16[64,128]{1,0:T(8,128)(2,1)} %bitcast.6), custom_call_target="tpu_custom_call" | custom-call | tf_op jit(solution)/shard_map/pallas_call | solution.py:206
  91.3 1.7 %broadcast_subtract_fusion = f32[32,8,256]{2,1,0:T(8,128)} fusion(f32[32,8,256]{2,1,0:T(8,128)} %get-tuple-element.4, f32[8]{0:T(128)} %bitcast.7), kind=kLoop, calls=%fused_computation | loop fusion | flops 65536 | bytes 524320 | tf_op jit(solution)/shard_map/sub | solution.py:238
  93.0 1.1 %copy.7 = f32[8]{0:T(128)} copy(f32[8]{0:T(128)} %bitcast.8) | data formatting | bytes 64
where the time goes:
time: 94.5 us; the launch traced here: 94.2 us
  Pallas kernels  90.7 us (96%)
  other arithmetic  1.74 us (2%)
  local copies, waits for them, and re-layouts  1.13 us (1%)
    pallas_call x1, Pallas kernels, per_device(): pl.pallas_call(functools.partial(kernel, n, m, block, chunks), in_specs=[...  90.7 us

commit v1 on v0

--- a/solution.py
+++ b/solution.py
@@ -18,6 +18,13 @@
 SLOTS = NODES * TOPS
 LINES = 2 * SLOTS
 MESH = pl.DeviceIdType.MESH
+F8 = jnp.float8_e4m3fn
+SLOT = 256
+PACK = 4
+DIGIT = 32
+BLOCKS = SUBLANES // 2
+FINE = 16.0
+H_SCALE = 256.0
 
 
 def partner(me, k, n):
@@ -30,7 +37,7 @@
     return out
 
 
-def kernel(
+def direct(
     n, m, block, chunks, bins_hbm, node_ref, g_ref, h_ref, out_ref, best_ref,
     bins_buf, high_ref, low_ref, g_all, h_all, acc_ref, stage, landed, row_best, feat_best,
     load_sem, send_sem, recv_sem, row_send, row_recv, feat_send, feat_recv,
@@ -192,19 +199,462 @@
     best_ref[...] = flat[:, :NODES]
 
 
+def regroup(
+    bins_hbm, node_ref, g_ref, h_ref, words_ref, gh_ref, keep_ref, last_ref,
+    bins, pieces, pattern, spots_v, spots_s, load_sem, spots_sem,
+):
+    f32, bf16, i32 = jnp.float32, jnp.bfloat16, jnp.int32
+    tiles = node_ref.shape[0]
+    groups, features = bins.shape[:2]
+    slots = words_ref.shape[0] // 2
+
+    def load(t):
+        return pltpu.make_async_copy(bins_hbm.at[pl.ds(t * features, features), :], bins.at[t], load_sem.at[t])
+
+    for t in range(groups):
+        load(t).start()
+    node = node_ref[...]
+    g = g_ref[...].astype(f32)
+    h = h_ref[...].astype(f32)
+    top = jnp.max(jnp.max(jnp.abs(g), axis=0, keepdims=True), axis=1, keepdims=True)
+    top = jnp.broadcast_to(top, (SUBLANES, LANES))
+    scale = jnp.ones((SUBLANES, LANES), f32)
+    back = jnp.ones((SUBLANES, LANES), f32)
+    for k in (32, 16, 8, 4, 2, 1):
+        fits = top * (scale * 2.0**k) <= 448.0
+        scale = jnp.where(fits, scale * 2.0**k, scale)
+        back = jnp.where(fits, back * 2.0**-k, back)
+
+    def split(x):
+        coarse = x.astype(F8).astype(f32)
+        return coarse, (x - coarse) * FINE
+
+    for i, piece in enumerate(split(g * scale[:1]) + split(h * H_SCALE)):
+        pieces[i] = piece
+
+    row = lax.broadcasted_iota(i32, (LANES, LANES), 0)
+    col = lax.broadcasted_iota(i32, (LANES, LANES), 1)
+    upper = jnp.where(row <= col, 1.0, 0.0).astype(bf16)
+    ones = jnp.ones((LANES, LANES), bf16)
+    above = lax.broadcasted_iota(i32, (tiles, tiles), 1) < lax.broadcasted_iota(i32, (tiles, tiles), 0)
+    lower = jnp.where(above, 1.0, 0.0).astype(bf16)
+    dot = functools.partial(jnp.dot, preferred_element_type=f32)
+    lane = lax.broadcasted_iota(i32, (tiles, LANES), 1)
+    slot = lax.broadcasted_iota(i32, keep_ref.shape, 0)
+    keep = jnp.ones(keep_ref.shape, f32)
+    base = jnp.zeros((1, LANES), i32)
+    last = jnp.zeros((1, LANES), i32)
+    dest = jnp.zeros((tiles, LANES), i32)
+    spots = jnp.zeros((tiles, LANES), i32)
+    for n in range(NODES):
+        hit = node == n
+        x = jnp.where(hit, 1.0, 0.0).astype(bf16)
+        rank = dot(x, upper).astype(i32)
+        count = dot(x, ones)
+        ahead = dot(lower, count.astype(bf16)).astype(i32)
+        count = count.astype(i32)
+        total = (ahead + count)[tiles - 1 : tiles]
+        start = ahead + base
+        dest = jnp.where(hit, start + rank - 1, dest)
+        spots = jnp.where(lane == n, start, jnp.where(lane == NODES + n, start + count, spots))
+        keep = jnp.where(slot * SLOT == base, 0.0, keep)
+        base = base + jnp.maximum((total + (SLOT - 1)) // SLOT, 1) * SLOT
+        last = jnp.where(lane[:1] == n, base // SLOT - 1, last)
+    keep_ref[...] = jnp.where(slot == slots, jnp.broadcast_to(back[:1], keep_ref.shape), keep)
+    last_ref[...] = last
+    spots_v[...] = spots
+    to_scalar = pltpu.make_async_copy(spots_v, spots_s, spots_sem)
+    to_scalar.start()
+
+    spot = dest & (LANES - 1)
+    sub = lax.broadcasted_iota(i32, (NODES, LANES), 0)
+    across = lax.broadcasted_iota(i32, (NODES, LANES), 1)
+    none = jnp.zeros((NODES, LANES), i32)
+    for b in range(0, tiles, 2):
+        left, right = [], []
+        for i in range(2):
+            here = jnp.where(jnp.broadcast_to(node[b + i : b + i + 1], (NODES, LANES)) == sub, across, 0)
+            left.append(jnp.concatenate([none] * i + [here] + [none] * (1 - i), 1))
+            right.append(jnp.where(jnp.broadcast_to(spot[b + i : b + i + 1], (LANES, LANES)) == row, 1.0, 0.0))
+        found = lax.dot_general(
+            jnp.concatenate(left, 0).astype(f32).astype(bf16),
+            jnp.concatenate(right, 1).astype(bf16),
+            (((1,), (1,)), ((), ())),
+            preferred_element_type=f32,
+        ).astype(i32)
+        pattern[b] = found[:NODES]
+        pattern[b + 1] = found[NODES:]
+    gh_ref[...] = jnp.zeros(gh_ref.shape, f32)
+    to_scalar.wait()
+    for t in range(groups):
+        load(t).wait()
+
+    def place(b, carry):
+        cols = pl.ds(pl.multiple_of(b * LANES, LANES), LANES)
+        words = []
+        for t in range(groups):
+            word = bins[t, :SUBLANES, cols]
+            for k in range(1, PACK):
+                word = word | lax.shift_left(bins[t, SUBLANES * k : SUBLANES * (k + 1), cols], 8 * k)
+            words.append(word)
+        piece = [jnp.broadcast_to(pieces[i, pl.ds(b, 1), :], (SUBLANES, LANES)) for i in range(4)]
+        gh = jnp.where(sub == 0, piece[0], jnp.where(sub == 1, piece[1], jnp.where(sub == 2, piece[2], piece[3])))
+        for n in range(NODES):
+            first = spots_s[b, n]
+            tile = lax.shift_right_logical(first, 7)
+            low = first & (LANES - 1)
+            high = low + spots_s[b, NODES + n] - first
+            source = jnp.broadcast_to(pattern[b, n : n + 1, :], (SUBLANES, LANES))
+            near = (across >= low) & (across < high)
+            far = across < high - LANES
+            for t in range(groups):
+                moved = jnp.take_along_axis(words[t], source, axis=1)
+                pltpu.store(words_ref.at[tile, t], moved, mask=near)
+                pltpu.store(words_ref.at[tile + 1, t], moved, mask=far)
+            moved = jnp.take_along_axis(gh, source, axis=1)
+            pltpu.store(gh_ref.at[tile], moved, mask=near)
+            pltpu.store(gh_ref.at[tile + 1], moved, mask=far)
+        return carry
+
+    lax.fori_loop(0, tiles, place, 0, unroll=8)
+
+
+def sweep(
+    n, m, words_hbm, gh_ref, keep_ref, last_ref, out_ref, best_ref,
+    words, keys, gh, snap, stage, near, relay, far, own, row_best, feat_best,
+    load_sem, near_send, near_recv, far_send, far_recv, row_send, row_recv, feat_send, feat_recv,
+):
+    f32 = jnp.float32
+    tiles = words.shape[1]
+    slots = tiles * LANES // SLOT
+    pairs = n // 2
+    me = lax.axis_index("row")
+    mine = lax.axis_index("feat")
+    chip, core = me // 2, me % 2
+
+    def to_chip(k):
+        return partner(chip, pairs - 1 - k, pairs)
+
+    def load(t):
+        group = 2 * to_chip(t // 2) + (t + 1 + core) % 2
+        return pltpu.make_async_copy(
+            words_hbm.at[pl.ds(0, tiles), group], words.at[t % 2], load_sem.at[t % 2]
+        )
+
+    def send_near(k, i):
+        return pltpu.make_async_remote_copy(
+            src_ref=stage.at[k, i],
+            dst_ref=near.at[k, i],
+            send_sem=near_send.at[k, i],
+            recv_sem=near_recv.at[k, i],
+            device_id={"row": 2 * chip + 1 - core},
+            device_id_type=MESH,
+        )
+
+    def send_far(k, i):
+        return pltpu.make_async_remote_copy(
+            src_ref=relay.at[k, i],
+            dst_ref=far.at[k, i],
+            send_sem=far_send.at[k, i],
+            recv_sem=far_recv.at[k, i],
+            device_id={"row": 2 * to_chip(k) + core},
+            device_id_type=MESH,
+        )
+
+    load(0).start()
+    barrier = pltpu.get_barrier_semaphore()
+    for k in range(1, n):
+        pl.semaphore_signal(barrier, inc=1, device_id={"row": (me + k) % n}, device_id_type=MESH)
+    for k in range(1, m):
+        pl.semaphore_signal(barrier, inc=1, device_id={"feat": (mine + k) % m}, device_id_type=MESH)
+    for p in range(4):
+        for q in range(tiles):
+            gh[p, :, q * LANES : (q + 1) * LANES] = jnp.broadcast_to(gh_ref[q, p : p + 1, :], (32, LANES)).astype(F8)
+    pl.semaphore_wait(barrier, n + m - 2)
+
+    wide = (32, SLOT)
+    down = lax.broadcasted_iota(jnp.int32, wide, 0) % SUBLANES
+    high_at = (down * DIGIT).astype(jnp.int8)
+    low_at = [(down + SUBLANES * j).astype(jnp.int8) for j in range(4)]
+    zero, one = jnp.zeros(wide, F8), jnp.ones(wide, F8)
+    lane = lax.broadcasted_iota(jnp.int32, (SUBLANES, LANES), 1)
+    sub = lax.broadcasted_iota(jnp.int32, (SUBLANES, LANES), 0)
+    byte = (lane // SUBLANES) % PACK
+    of = [byte == f for f in range(PACK - 1)]
+    g_back = jnp.broadcast_to(keep_ref[slots : slots + 1, :], (SUBLANES, LANES))
+    h_back = jnp.full((SUBLANES, LANES), 1.0 / H_SCALE, f32)
+
+    def unpack(t):
+        load(t).wait()
+
+        @pl.when(t + 1 < n)
+        def _():
+            load(t + 1).start()
+
+        for q in range(tiles):
+            word = words[t % 2, q]
+            for k in range(PACK):
+                keys[k, :, q * LANES : (q + 1) * LANES] = lax.shift_right_logical(word, 8 * k)
+
+    def one_hots(w, cols):
+        rows = [jnp.broadcast_to(keys[k, pl.ds(w, 1), cols], (SUBLANES, SLOT)) for k in range(PACK)]
+        key = jnp.concatenate(rows, 0).astype(jnp.int8)
+        low, high = key & jnp.int8(DIGIT - 1), key & jnp.int8(-DIGIT)
+        apart = high != high_at
+        left = [jnp.where(apart, zero, gh[p, :, cols]) for p in range(4)]
+        right = [jnp.where(low != low_at[j], zero, one) for j in range(4)]
+        return left, right
+
+    def block(i):
+        total = [jnp.zeros((SUBLANES, LANES), f32) for _ in range(4)]
+        for s in range(slots):
+            cols = slice(s * SLOT, (s + 1) * SLOT)
+            left0, right0 = one_hots(2 * i, cols)
+            left1, right1 = one_hots(2 * i + 1, cols)
+            found = lax.dot_general(
+                jnp.concatenate(left0 + left1, 0),
+                jnp.concatenate(right0 + right1, 0),
+                (((1,), (1,)), ((), ())),
+                preferred_element_type=f32,
+            )
+            kept = jnp.broadcast_to(keep_ref[s : s + 1, :], (SUBLANES, LANES))
+            for q in range(2):
+                square = found[q * LANES : (q + 1) * LANES, q * LANES : (q + 1) * LANES]
+                dense = []
+                for p in range(4):
+                    part = [square[32 * p + 8 * f : 32 * p + 8 * f + 8] for f in range(PACK)]
+                    dense.append(jnp.where(of[0], part[0], jnp.where(of[1], part[1], jnp.where(of[2], part[2], part[3]))))
+                for v in range(2):
+                    at = 2 * q + v
+                    total[at] = total[at] * kept + (dense[2 * v] + dense[2 * v + 1] * (1.0 / FINE))
+                    snap[s, at] = total[at]
+
+    def hist(node, at):
+        return snap[last_ref[0, node], at] * (h_back if at % 2 else g_back)
+
+    def pair(k, carry):
+        unpack(2 * k)
+
+        def give(i, c):
+            @pl.when(i > 0)
+            def _():
+                send_near(k, i - 1).start()
+
+            @pl.when((i == 0) & (k > 0))
+            def _():
+                send_far(k - 1, BLOCKS - 1).start()
+
+            block(i)
+            for node in range(NODES):
+                for at in range(4):
+                    stage[k, i, node, at] = hist(node, at)
+            return c
+
+        lax.fori_loop(0, BLOCKS, give, 0)
+        unpack(2 * k + 1)
+
+        def hold(i, c):
+            @pl.when(i == 0)
+            def _():
+                send_near(k, BLOCKS - 1).start()
+
+            @pl.when((i > 0) & (k < pairs - 1))
+            def _():
+                send_far(k, i - 1).start()
+
+            block(i)
+            send_near(k, i).wait_recv()
+
+            @pl.when(k < pairs - 1)
+            def _():
+                for node in range(NODES):
+                    for at in range(4):
+                        relay[k, i, node, at] = hist(node, at) + near[k, i, node, at]
+
+            @pl.when(k == pairs - 1)
+            def _():
+                for node in range(NODES):
+                    for at in range(4):
+                        own[i, node, at] = hist(node, at) + near[k, i, node, at]
+
+            return c
+
+        lax.fori_loop(0, BLOCKS, hold, 0)
+        return carry
+
+    lax.fori_loop(0, pairs, pair, 0)
+
+    def take(x, index):
+        return jnp.take_along_axis(x, index, axis=1)
+
+    tens, units = lane // (SUBLANES * PACK), lane % SUBLANES
+    end_of_run = lane - units + (SUBLANES - 1)
+    end_of_row = (LANES - DIGIT) + byte * SUBLANES + (SUBLANES - 1)
+
+    def running(x):
+        for shift in (1, 2, 4):
+            x = x + jnp.where(units >= shift, pltpu.roll(x, shift, 1), 0.0)
+        run = take(x, end_of_run)
+        for j in range(1, 4):
+            x = x + jnp.where(tens >= j, pltpu.roll(run, j * DIGIT, 1), 0.0)
+        row = take(x, end_of_row)
+        whole = row
+        for shift in (1, 2, 4):
+            whole = whole + jnp.where(sub >= shift, pltpu.roll(whole, shift, 0), 0.0)
+        return x + (whole - row), jnp.broadcast_to(whole[SUBLANES - 1 :], whole.shape)
+
+    def finish(i, best):
+        for k in range(pairs - 1):
+            send_far(k, i).wait_recv()
+        for q in range(2):
+            gains = []
+            for node in range(NODES):
+                sums = []
+                for at in (2 * q, 2 * q + 1):
+                    x = own[i, node, at]
+                    for k in range(pairs - 1):
+                        x = x + far[k, i, node, at]
+                    sums.append(running(x))
+                (gl, gt), (hl, ht) = sums
+                gain = gl * gl / (hl + 1.0)
+                gain = gain + (gt - gl) * (gt - gl) / (ht - hl + 1.0)
+                gains.append(gain - gt * gt / (ht + 1.0))
+            best = jnp.maximum(best, jnp.stack([jnp.max(x, axis=0) for x in gains], 0))
+            turned = jnp.swapaxes(jnp.stack(gains, 0), 0, 1)
+            for f in range(PACK):
+                source = ((lane // SUBLANES) % 4) * DIGIT + f * SUBLANES + units
+                for t in range(TOPS):
+                    part = [take(turned[4 * t + j], source) for j in range(4)]
+                    line = jnp.where(tens == 0, part[0], jnp.where(tens == 1, part[1], jnp.where(tens == 2, part[2], part[3])))
+                    out_ref[SUBLANES * f + 2 * i + q, :, t * LANES : (t + 1) * LANES] = line
+        return best
+
+    top_gain = lax.fori_loop(0, BLOCKS, finish, jnp.full((NODES, LANES), -jnp.inf, f32))
+
+    def exchange(value, slots, count, axis, index, sems, arrived):
+        slots[0] = jnp.broadcast_to(jnp.max(value, axis=1, keepdims=True), (NODES, LANES))
+        copies = []
+        for k in range(1, count):
+            copies.append(
+                pltpu.make_async_remote_copy(
+                    src_ref=slots.at[0],
+                    dst_ref=slots.at[k],
+                    send_sem=sems.at[k - 1],
+                    recv_sem=arrived.at[k - 1],
+                    device_id={axis: (index + k) % count},
+                    device_id_type=MESH,
+                )
+            )
+            copies[-1].start()
+        for copy in copies:
+            copy.wait()
+        best = slots[0]
+        for k in range(1, count):
+            best = jnp.maximum(best, slots[k])
+        return best
+
+    best = exchange(top_gain, row_best, n, "row", me, row_send, row_recv)
+    best = exchange(best, feat_best, m, "feat", mine, feat_send, feat_recv)
+    flat = jnp.max(jnp.where(lane == sub, best, -jnp.inf), axis=0, keepdims=True)
+    best_ref[...] = flat[:, :NODES]
+
+    def drain(k, carry):
+        for i in range(BLOCKS):
+            send_near(k, i).wait_send()
+
+            @pl.when(k < pairs - 1)
+            def _():
+                send_far(k, i).wait_send()
+
+        return carry
+
+    lax.fori_loop(0, pairs, drain, 0)
+
+
+def grouped(n, m, bins, grads, hess, node):
+    features, rows = bins.shape
+    groups, tiles = features // 32, rows // LANES
+    slots = rows // SLOT + NODES - 1
+    held = 2 * slots
+    vmem = pl.BlockSpec(memory_space=pltpu.VMEM)
+    smem = pl.BlockSpec(memory_space=pltpu.SMEM)
+    hbm = pl.BlockSpec(memory_space=pl.ANY)
+    words, gh, keep, last = pl.pallas_call(
+        regroup,
+        in_specs=[hbm, vmem, vmem, vmem],
+        out_specs=(vmem, vmem, vmem, vmem),
+        out_shape=(
+            jax.ShapeDtypeStruct((held + 1, groups, SUBLANES, LANES), jnp.int32),
+            jax.ShapeDtypeStruct((held + 1, SUBLANES, LANES), jnp.float32),
+            jax.ShapeDtypeStruct((-(-(slots + 1) // SUBLANES) * SUBLANES, LANES), jnp.float32),
+            jax.ShapeDtypeStruct((1, LANES), jnp.int32),
+        ),
+        scratch_shapes=[
+            pltpu.VMEM((groups, 32, rows), jnp.int32),
+            pltpu.VMEM((4, tiles, LANES), jnp.float32),
+            pltpu.VMEM((tiles, NODES, LANES), jnp.int32),
+            pltpu.VMEM((tiles, LANES), jnp.int32),
+            pltpu.SMEM((tiles, LANES), jnp.int32),
+            pltpu.SemaphoreType.DMA((groups,)),
+            pltpu.SemaphoreType.DMA,
+        ],
+        compiler_params=pltpu.CompilerParams(vmem_limit_bytes=56 << 20),
+    )(bins, node.reshape(-1, LANES), grads.reshape(-1, LANES), hess.reshape(-1, LANES))
+    pairs = n // 2
+    piece = (BLOCKS, NODES, 4, SUBLANES, LANES)
+    out, best = pl.pallas_call(
+        functools.partial(sweep, n, m),
+        in_specs=[hbm, vmem, vmem, smem],
+        out_specs=(vmem, vmem),
+        out_shape=(
+            jax.ShapeDtypeStruct((32, NODES, BINS), jnp.float32),
+            jax.ShapeDtypeStruct((1, NODES), jnp.float32),
+        ),
+        scratch_shapes=[
+            pltpu.VMEM((2, held, SUBLANES, LANES), jnp.int32),
+            pltpu.VMEM((PACK, SUBLANES, held * LANES), jnp.int32),
+            pltpu.VMEM((4, 32, held * LANES), F8),
+            pltpu.VMEM((slots, 4, SUBLANES, LANES), jnp.float32),
+            pltpu.VMEM((pairs,) + piece, jnp.float32),
+            pltpu.VMEM((pairs,) + piece, jnp.float32),
+            pltpu.VMEM((pairs - 1,) + piece, jnp.float32),
+            pltpu.VMEM((pairs - 1,) + piece, jnp.float32),
+            pltpu.VMEM(piece, jnp.float32),
+            pltpu.VMEM((n, NODES, LANES), jnp.float32),
+            pltpu.VMEM((m, NODES, LANES), jnp.float32),
+            pltpu.SemaphoreType.DMA((2,)),
+            pltpu.SemaphoreType.DMA((pairs, BLOCKS)),
+            pltpu.SemaphoreType.DMA((pairs, BLOCKS)),
+            pltpu.SemaphoreType.DMA((pairs - 1, BLOCKS)),
+            pltpu.SemaphoreType.DMA((pairs - 1, BLOCKS)),
+            pltpu.SemaphoreType.DMA((n - 1,)),
+            pltpu.SemaphoreType.DMA((n - 1,)),
+            pltpu.SemaphoreType.DMA((m - 1,)),
+            pltpu.SemaphoreType.DMA((m - 1,)),
+        ],
+        compiler_params=pltpu.CompilerParams(
+            collective_id=0, has_side_effects=True, vmem_limit_bytes=56 << 20
+        ),
+    )(words, gh, keep, last)
+    best = best.reshape(NODES)
+    return out - best[None, :, None], best
+
+
 def solution(mesh):
     n, m = mesh.shape["row"], mesh.shape["feat"]
 
     def per_device(bins, grads, hess, node):
         features, rows = bins.shape
         own = features // n
+        if own == 32 and n % 2 == 0 and n > 2 and rows % (2 * SLOT) == 0:
+            return grouped(n, m, bins, grads, hess, node)
         block = own if own < SUBLANES else next(b for b in (2 * SUBLANES, SUBLANES) if own % b == 0)
         held = max(block, SUBLANES)
         chunks = own // block
         vmem = pl.BlockSpec(memory_space=pltpu.VMEM)
         piece = (block, LINES, LANES)
         out, best = pl.pallas_call(
-            functools.partial(kernel, n, m, block, chunks),
+            functools.partial(direct, n, m, block, chunks),
             in_specs=[pl.BlockSpec(memory_space=pl.ANY), vmem, vmem, vmem],
             out_specs=(vmem, vmem),
             out_shape=(

time: 94.5 us -> 64.6 us (0.68)
  Pallas kernels: 90.7 us -> 60.9 us
    pallas_call x1 -> x2, Pallas kernels: 90.7 us -> 60.9 us  [the longest x1 48 us: grouped(): pl.pallas_call(functools.partial(sweep, n, m), in_specs=[hbm, vmem, vmem,...]
where the time goes in v1:
time: 64.6 us; the launch traced here: 64.4 us
  Pallas kernels  60.9 us (94%)
  other arithmetic  1.74 us (3%)
  local copies, waits for them, and re-layouts  1.09 us (2%)
  between operations  0.65 us (1%)
    pallas_call x1, Pallas kernels, grouped(): pl.pallas_call(functools.partial(sweep, n, m), in_specs=[hbm, vmem, vmem,...  48 us
    pallas_call x1, Pallas kernels, grouped(): pl.pallas_call(regroup, in_specs=[hbm, vmem, vmem, vmem], out_specs=(vmem...  12.9 us
    sub x1, other arithmetic, grouped(): return (out - best[None, :, None], best)  1.74 us

profile of v1, /device:TPU:0, one launch (start us, length us, event | category | flops | bytes accessed | tf_op | source)
XLA Modules:
  0.0 64.4 jit_solution(14690660204532860280)
XLA Ops:
  0.6 12.9 %shard_map.59 = (s32[79,8,8,128]{3,2,1,0:T(8,128)}, f32[79,8,128]{2,1,0:T(8,128)}, f32[40,128]{1,0:T(8,128)}, s32[1,128]{1,0:T(1,128)}) custom-call(s32[256,8192]{1,0:T(8,128)} %bins_hbm.1, s32[64,128]{1,0:T(8,128)} %bitcast.4, bf16[64,128]{1,0:T(8,128)(2,1)} %bitcast.5, bf16[64,128]{1,0:T(8,128)(2,1)} %bitcast.6), custom_call_target="tpu_custom_call" | custom-call | tf_op jit(solution)/shard_map/pallas_call | solution.py:582
  13.5 48.0 %shard_map.60 = (f32[32,8,256]{2,1,0:T(8,128)}, f32[1,8]{1,0:T(1,128)}) custom-call(s32[79,8,8,128]{3,2,1,0:T(8,128)} %get-tuple-element.8.words_hbm, f32[79,8,128]{2,1,0:T(8,128)} %get-tuple-element.9.gh_ref, f32[40,128]{1,0:T(8,128)} %get-tuple-element.10.keep_ref, s32[1,128]{1,0:T(1,128)} %get-tuple-element.11.last_ref), custom_call_target="tpu_custom_call" | custom-call | tf_op jit(solution)/shard_map/pallas_call | solution.py:605
  61.5 1.7 %broadcast_subtract_fusion = f32[32,8,256]{2,1,0:T(8,128)} fusion(f32[32,8,256]{2,1,0:T(8,128)} %get-tuple-element.12, f32[8]{0:T(128)} %bitcast.7), kind=kLoop, calls=%fused_computation | loop fusion | flops 65536 | bytes 524320 | tf_op jit(solution)/shard_map/sub | solution.py:640
  63.3 1.1 %copy.7 = f32[8]{0:T(128)} copy(f32[8]{0:T(128)} %bitcast.8) | data formatting | bytes 64

commit v2 on v1

--- a/solution.py
+++ b/solution.py
@@ -23,8 +23,6 @@
 PACK = 4
 DIGIT = 32
 BLOCKS = SUBLANES // 2
-FINE = 16.0
-H_SCALE = 256.0
 
 
 def partner(me, k, n):
@@ -206,7 +204,6 @@
     f32, bf16, i32 = jnp.float32, jnp.bfloat16, jnp.int32
     tiles = node_ref.shape[0]
     groups, features = bins.shape[:2]
-    slots = words_ref.shape[0] // 2
 
     def load(t):
         return pltpu.make_async_copy(bins_hbm.at[pl.ds(t * features, features), :], bins.at[t], load_sem.at[t])
@@ -214,24 +211,8 @@
     for t in range(groups):
         load(t).start()
     node = node_ref[...]
-    g = g_ref[...].astype(f32)
-    h = h_ref[...].astype(f32)
-    top = jnp.max(jnp.max(jnp.abs(g), axis=0, keepdims=True), axis=1, keepdims=True)
-    top = jnp.broadcast_to(top, (SUBLANES, LANES))
-    scale = jnp.ones((SUBLANES, LANES), f32)
-    back = jnp.ones((SUBLANES, LANES), f32)
-    for k in (32, 16, 8, 4, 2, 1):
-        fits = top * (scale * 2.0**k) <= 448.0
-        scale = jnp.where(fits, scale * 2.0**k, scale)
-        back = jnp.where(fits, back * 2.0**-k, back)
-
-    def split(x):
-        coarse = x.astype(F8).astype(f32)
-        return coarse, (x - coarse) * FINE
-
-    for i, piece in enumerate(split(g * scale[:1]) + split(h * H_SCALE)):
-        pieces[i] = piece
-
+    pieces[0] = g_ref[...].astype(f32)
+    pieces[1] = h_ref[...].astype(f32)
     row = lax.broadcasted_iota(i32, (LANES, LANES), 0)
     col = lax.broadcasted_iota(i32, (LANES, LANES), 1)
     upper = jnp.where(row <= col, 1.0, 0.0).astype(bf16)
@@ -260,7 +241,7 @@
         keep = jnp.where(slot * SLOT == base, 0.0, keep)
         base = base + jnp.maximum((total + (SLOT - 1)) // SLOT, 1) * SLOT
         last = jnp.where(lane[:1] == n, base // SLOT - 1, last)
-    keep_ref[...] = jnp.where(slot == slots, jnp.broadcast_to(back[:1], keep_ref.shape), keep)
+    keep_ref[...] = keep
     last_ref[...] = last
     spots_v[...] = spots
     to_scalar = pltpu.make_async_copy(spots_v, spots_s, spots_sem)
@@ -297,8 +278,8 @@
             for k in range(1, PACK):
                 word = word | lax.shift_left(bins[t, SUBLANES * k : SUBLANES * (k + 1), cols], 8 * k)
             words.append(word)
-        piece = [jnp.broadcast_to(pieces[i, pl.ds(b, 1), :], (SUBLANES, LANES)) for i in range(4)]
-        gh = jnp.where(sub == 0, piece[0], jnp.where(sub == 1, piece[1], jnp.where(sub == 2, piece[2], piece[3])))
+        piece = [jnp.broadcast_to(pieces[i, pl.ds(b, 1), :], (SUBLANES, LANES)) for i in range(2)]
+        gh = jnp.where(sub == 0, piece[0], piece[1])
         for n in range(NODES):
             first = spots_s[b, n]
             tile = lax.shift_right_logical(first, 7)
@@ -367,23 +348,21 @@
         pl.semaphore_signal(barrier, inc=1, device_id={"row": (me + k) % n}, device_id_type=MESH)
     for k in range(1, m):
         pl.semaphore_signal(barrier, inc=1, device_id={"feat": (mine + k) % m}, device_id_type=MESH)
-    for p in range(4):
+    for p in range(2):
         for q in range(tiles):
-            gh[p, :, q * LANES : (q + 1) * LANES] = jnp.broadcast_to(gh_ref[q, p : p + 1, :], (32, LANES)).astype(F8)
+            gh[p, :, q * LANES : (q + 1) * LANES] = jnp.broadcast_to(gh_ref[q, p : p + 1, :], (16, LANES)).astype(jnp.bfloat16)
     pl.semaphore_wait(barrier, n + m - 2)
 
     wide = (32, SLOT)
     down = lax.broadcasted_iota(jnp.int32, wide, 0) % SUBLANES
-    high_at = (down * DIGIT).astype(jnp.int8)
+    high_at = (down[:16] * DIGIT).astype(jnp.int16)
     low_at = [(down + SUBLANES * j).astype(jnp.int8) for j in range(4)]
     zero, one = jnp.zeros(wide, F8), jnp.ones(wide, F8)
+    nil = jnp.zeros((16, SLOT), jnp.bfloat16)
     lane = lax.broadcasted_iota(jnp.int32, (SUBLANES, LANES), 1)
     sub = lax.broadcasted_iota(jnp.int32, (SUBLANES, LANES), 0)
     byte = (lane // SUBLANES) % PACK
     of = [byte == f for f in range(PACK - 1)]
-    g_back = jnp.broadcast_to(keep_ref[slots : slots + 1, :], (SUBLANES, LANES))
-    h_back = jnp.full((SUBLANES, LANES), 1.0 / H_SCALE, f32)
-
     def unpack(t):
         load(t).wait()
 
@@ -398,10 +377,12 @@
 
     def one_hots(w, cols):
         rows = [jnp.broadcast_to(keys[k, pl.ds(w, 1), cols], (SUBLANES, SLOT)) for k in range(PACK)]
-        key = jnp.concatenate(rows, 0).astype(jnp.int8)
-        low, high = key & jnp.int8(DIGIT - 1), key & jnp.int8(-DIGIT)
-        apart = high != high_at
-        left = [jnp.where(apart, zero, gh[p, :, cols]) for p in range(4)]
+        twos = [jnp.concatenate(rows[i : i + 2], 0).astype(jnp.int16) for i in (0, 2)]
+        low = jnp.concatenate(rows, 0).astype(jnp.int8) & jnp.int8(DIGIT - 1)
+        left = []
+        for two in twos:
+            apart = (two & jnp.int16(BINS - DIGIT)) != high_at
+            left += [jnp.where(apart, nil, gh[v, :, cols]) for v in range(2)]
         right = [jnp.where(low != low_at[j], zero, one) for j in range(4)]
         return left, right
 
@@ -419,18 +400,16 @@
             )
             kept = jnp.broadcast_to(keep_ref[s : s + 1, :], (SUBLANES, LANES))
             for q in range(2):
-                square = found[q * LANES : (q + 1) * LANES, q * LANES : (q + 1) * LANES]
-                dense = []
-                for p in range(4):
-                    part = [square[32 * p + 8 * f : 32 * p + 8 * f + 8] for f in range(PACK)]
-                    dense.append(jnp.where(of[0], part[0], jnp.where(of[1], part[1], jnp.where(of[2], part[2], part[3]))))
+                square = found[64 * q : 64 * (q + 1), q * LANES : (q + 1) * LANES]
                 for v in range(2):
+                    part = [square[at : at + SUBLANES] for at in (16 * v, 16 * v + 8, 16 * v + 32, 16 * v + 40)]
+                    dense = jnp.where(of[0], part[0], jnp.where(of[1], part[1], jnp.where(of[2], part[2], part[3])))
                     at = 2 * q + v
-                    total[at] = total[at] * kept + (dense[2 * v] + dense[2 * v + 1] * (1.0 / FINE))
+                    total[at] = total[at] * kept + dense
                     snap[s, at] = total[at]
 
     def hist(node, at):
-        return snap[last_ref[0, node], at] * (h_back if at % 2 else g_back)
+        return snap[last_ref[0, node], at]
 
     def pair(k, carry):
         unpack(2 * k)
@@ -586,12 +565,12 @@
         out_shape=(
             jax.ShapeDtypeStruct((held + 1, groups, SUBLANES, LANES), jnp.int32),
             jax.ShapeDtypeStruct((held + 1, SUBLANES, LANES), jnp.float32),
-            jax.ShapeDtypeStruct((-(-(slots + 1) // SUBLANES) * SUBLANES, LANES), jnp.float32),
+            jax.ShapeDtypeStruct((-(-slots // SUBLANES) * SUBLANES, LANES), jnp.float32),
             jax.ShapeDtypeStruct((1, LANES), jnp.int32),
         ),
         scratch_shapes=[
             pltpu.VMEM((groups, 32, rows), jnp.int32),
-            pltpu.VMEM((4, tiles, LANES), jnp.float32),
+            pltpu.VMEM((2, tiles, LANES), jnp.float32),
             pltpu.VMEM((tiles, NODES, LANES), jnp.int32),
             pltpu.VMEM((tiles, LANES), jnp.int32),
             pltpu.SMEM((tiles, LANES), jnp.int32),
@@ -613,7 +592,7 @@
         scratch_shapes=[
             pltpu.VMEM((2, held, SUBLANES, LANES), jnp.int32),
             pltpu.VMEM((PACK, SUBLANES, held * LANES), jnp.int32),
-            pltpu.VMEM((4, 32, held * LANES), F8),
+            pltpu.VMEM((2, 16, held * LANES), jnp.bfloat16),
             pltpu.VMEM((slots, 4, SUBLANES, LANES), jnp.float32),
             pltpu.VMEM((pairs,) + piece, jnp.float32),
             pltpu.VMEM((pairs,) + piece, jnp.float32),

time: 64.6 us -> 64.8 us (level)
  no operation moved by 1% of the time
where the time goes in v2:
time: 64.8 us; the launch traced here: 64.5 us
  Pallas kernels  61 us (94%)
  other arithmetic  1.74 us (3%)
  local copies, waits for them, and re-layouts  1.09 us (2%)
  between operations  0.65 us (1%)
    pallas_call x1, Pallas kernels, grouped(): pl.pallas_call(functools.partial(sweep, n, m), in_specs=[hbm, vmem, vmem,...  48.1 us
    pallas_call x1, Pallas kernels, grouped(): pl.pallas_call(regroup, in_specs=[hbm, vmem, vmem, vmem], out_specs=(vmem...  12.9 us
    sub x1, other arithmetic, grouped(): return (out - best[None, :, None], best)  1.74 us

profile of v2, /device:TPU:0, one launch (start us, length us, event | category | flops | bytes accessed | tf_op | source)
XLA Modules:
  0.0 64.5 jit_solution(9481867074298739999)
XLA Ops:
  0.6 12.9 %shard_map.59 = (s32[79,8,8,128]{3,2,1,0:T(8,128)}, f32[79,8,128]{2,1,0:T(8,128)}, f32[40,128]{1,0:T(8,128)}, s32[1,128]{1,0:T(1,128)}) custom-call(s32[256,8192]{1,0:T(8,128)} %bins_hbm.1, s32[64,128]{1,0:T(8,128)} %bitcast.4, bf16[64,128]{1,0:T(8,128)(2,1)} %bitcast.5, bf16[64,128]{1,0:T(8,128)(2,1)} %bitcast.6), custom_call_target="tpu_custom_call" | custom-call | tf_op jit(solution)/shard_map/pallas_call | solution.py:561
  13.5 48.1 %shard_map.60 = (f32[32,8,256]{2,1,0:T(8,128)}, f32[1,8]{1,0:T(1,128)}) custom-call(s32[79,8,8,128]{3,2,1,0:T(8,128)} %get-tuple-element.8.words_hbm, f32[79,8,128]{2,1,0:T(8,128)} %get-tuple-element.9.gh_ref, f32[40,128]{1,0:T(8,128)} %get-tuple-element.10.keep_ref, s32[1,128]{1,0:T(1,128)} %get-tuple-element.11.last_ref), custom_call_target="tpu_custom_call" | custom-call | tf_op jit(solution)/shard_map/pallas_call | solution.py:584
  61.7 1.7 %broadcast_subtract_fusion = f32[32,8,256]{2,1,0:T(8,128)} fusion(f32[32,8,256]{2,1,0:T(8,128)} %get-tuple-element.12, f32[8]{0:T(128)} %bitcast.7), kind=kLoop, calls=%fused_computation | loop fusion | flops 65536 | bytes 524320 | tf_op jit(solution)/shard_map/sub | solution.py:619
  63.4 1.1 %copy.7 = f32[8]{0:T(128)} copy(f32[8]{0:T(128)} %bitcast.8) | data formatting | bytes 64

commit v3 on v2

--- a/solution.py
+++ b/solution.py
@@ -21,6 +21,7 @@
 F8 = jnp.float8_e4m3fn
 SLOT = 256
 PACK = 4
+CHUNK = 8
 DIGIT = 32
 BLOCKS = SUBLANES // 2
 
@@ -197,19 +198,25 @@
     best_ref[...] = flat[:, :NODES]
 
 
+def take(x, index):
+    return jnp.take_along_axis(x, index, axis=1, mode="promise_in_bounds")
+
+
 def regroup(
     bins_hbm, node_ref, g_ref, h_ref, words_ref, gh_ref, keep_ref, last_ref,
     bins, pieces, pattern, spots_v, spots_s, load_sem, spots_sem,
 ):
     f32, bf16, i32 = jnp.float32, jnp.bfloat16, jnp.int32
     tiles = node_ref.shape[0]
-    groups, features = bins.shape[:2]
-
-    def load(t):
-        return pltpu.make_async_copy(bins_hbm.at[pl.ds(t * features, features), :], bins.at[t], load_sem.at[t])
-
-    for t in range(groups):
-        load(t).start()
+    groups = bins.shape[0] // 32
+    chunks = tiles // CHUNK
+
+    def load(c):
+        cols = pl.ds(pl.multiple_of(c * (CHUNK * LANES), CHUNK * LANES), CHUNK * LANES)
+        return pltpu.make_async_copy(bins_hbm.at[:, cols], bins.at[:, cols], load_sem.at[c])
+
+    for c in range(chunks):
+        load(c).start()
     node = node_ref[...]
     pieces[0] = g_ref[...].astype(f32)
     pieces[1] = h_ref[...].astype(f32)
@@ -267,16 +274,14 @@
         pattern[b + 1] = found[NODES:]
     gh_ref[...] = jnp.zeros(gh_ref.shape, f32)
     to_scalar.wait()
-    for t in range(groups):
-        load(t).wait()
-
-    def place(b, carry):
+
+    def place(b):
         cols = pl.ds(pl.multiple_of(b * LANES, LANES), LANES)
         words = []
         for t in range(groups):
-            word = bins[t, :SUBLANES, cols]
+            word = bins[32 * t : 32 * t + SUBLANES, cols]
             for k in range(1, PACK):
-                word = word | lax.shift_left(bins[t, SUBLANES * k : SUBLANES * (k + 1), cols], 8 * k)
+                word = word | lax.shift_left(bins[32 * t + SUBLANES * k : 32 * t + SUBLANES * (k + 1), cols], 8 * k)
             words.append(word)
         piece = [jnp.broadcast_to(pieces[i, pl.ds(b, 1), :], (SUBLANES, LANES)) for i in range(2)]
         gh = jnp.where(sub == 0, piece[0], piece[1])
@@ -289,20 +294,25 @@
             near = (across >= low) & (across < high)
             far = across < high - LANES
             for t in range(groups):
-                moved = jnp.take_along_axis(words[t], source, axis=1)
+                moved = take(words[t], source)
                 pltpu.store(words_ref.at[tile, t], moved, mask=near)
                 pltpu.store(words_ref.at[tile + 1, t], moved, mask=far)
-            moved = jnp.take_along_axis(gh, source, axis=1)
+            moved = take(gh, source)
             pltpu.store(gh_ref.at[tile], moved, mask=near)
             pltpu.store(gh_ref.at[tile + 1], moved, mask=far)
+
+    def chunk(c, carry):
+        load(c).wait()
+        for j in range(CHUNK):
+            place(c * CHUNK + j)
         return carry
 
-    lax.fori_loop(0, tiles, place, 0, unroll=8)
+    lax.fori_loop(0, chunks, chunk, 0)
 
 
 def sweep(
     n, m, words_hbm, gh_ref, keep_ref, last_ref, out_ref, best_ref,
-    words, keys, gh, snap, stage, near, relay, far, own, row_best, feat_best,
+    words, keys, gh, snap, stage, near, relay, far, row_best, feat_best,
     load_sem, near_send, near_recv, far_send, far_recv, row_send, row_recv, feat_send, feat_recv,
 ):
     f32 = jnp.float32
@@ -406,65 +416,53 @@
                     dense = jnp.where(of[0], part[0], jnp.where(of[1], part[1], jnp.where(of[2], part[2], part[3])))
                     at = 2 * q + v
                     total[at] = total[at] * kept + dense
-                    snap[s, at] = total[at]
-
-    def hist(node, at):
-        return snap[last_ref[0, node], at]
+                    snap[i % 2, s, at] = total[at]
+
+    def store(ref, k, i):
+        for node in range(NODES):
+            for at in range(4):
+                ref[k, i, node, at] = snap[i % 2, last_ref[0, node], at]
+
+    def merge(k, i):
+        send_near(k, i).wait_recv()
+        for node in range(NODES):
+            for at in range(4):
+                relay[k, i, node, at] += near[k, i, node, at]
 
     def pair(k, carry):
         unpack(2 * k)
 
-        def give(i, c):
-            @pl.when(i > 0)
-            def _():
+        @pl.when(k > 0)
+        def _():
+            for i in range(2, BLOCKS):
+                send_far(k - 1, i).start()
+
+        for i in range(BLOCKS):
+            block(i)
+            if i > 0:
                 send_near(k, i - 1).start()
-
-            @pl.when((i == 0) & (k > 0))
-            def _():
-                send_far(k - 1, BLOCKS - 1).start()
+            store(stage, k, i)
+        unpack(2 * k + 1)
+        for i in range(BLOCKS):
+            if i == 0:
+                send_near(k, BLOCKS - 1).start()
+            if i == BLOCKS - 1:
+
+                @pl.when(k < pairs - 1)
+                def _():
+                    for j in range(2):
+                        send_far(k, j).start()
 
             block(i)
-            for node in range(NODES):
-                for at in range(4):
-                    stage[k, i, node, at] = hist(node, at)
-            return c
-
-        lax.fori_loop(0, BLOCKS, give, 0)
-        unpack(2 * k + 1)
-
-        def hold(i, c):
-            @pl.when(i == 0)
-            def _():
-                send_near(k, BLOCKS - 1).start()
-
-            @pl.when((i > 0) & (k < pairs - 1))
-            def _():
-                send_far(k, i - 1).start()
-
-            block(i)
-            send_near(k, i).wait_recv()
-
-            @pl.when(k < pairs - 1)
-            def _():
-                for node in range(NODES):
-                    for at in range(4):
-                        relay[k, i, node, at] = hist(node, at) + near[k, i, node, at]
-
-            @pl.when(k == pairs - 1)
-            def _():
-                for node in range(NODES):
-                    for at in range(4):
-                        own[i, node, at] = hist(node, at) + near[k, i, node, at]
-
-            return c
-
-        lax.fori_loop(0, BLOCKS, hold, 0)
+            store(relay, k, i)
+            if i == 1:
+                merge(k, 0)
+                merge(k, 1)
+        for i in range(2, BLOCKS):
+            merge(k, i)
         return carry
 
     lax.fori_loop(0, pairs, pair, 0)
-
-    def take(x, index):
-        return jnp.take_along_axis(x, index, axis=1)
 
     tens, units = lane // (SUBLANES * PACK), lane % SUBLANES
     end_of_run = lane - units + (SUBLANES - 1)
@@ -490,7 +488,7 @@
             for node in range(NODES):
                 sums = []
                 for at in (2 * q, 2 * q + 1):
-                    x = own[i, node, at]
+                    x = relay[pairs - 1, i, node, at]
                     for k in range(pairs - 1):
                         x = x + far[k, i, node, at]
                     sums.append(running(x))
@@ -569,12 +567,12 @@
             jax.ShapeDtypeStruct((1, LANES), jnp.int32),
         ),
         scratch_shapes=[
-            pltpu.VMEM((groups, 32, rows), jnp.int32),
+            pltpu.VMEM((features, rows), jnp.int32),
             pltpu.VMEM((2, tiles, LANES), jnp.float32),
             pltpu.VMEM((tiles, NODES, LANES), jnp.int32),
             pltpu.VMEM((tiles, LANES), jnp.int32),
             pltpu.SMEM((tiles, LANES), jnp.int32),
-            pltpu.SemaphoreType.DMA((groups,)),
+            pltpu.SemaphoreType.DMA((tiles // CHUNK,)),
             pltpu.SemaphoreType.DMA,
         ],
         compiler_params=pltpu.CompilerParams(vmem_limit_bytes=56 << 20),
@@ -593,12 +591,11 @@
             pltpu.VMEM((2, held, SUBLANES, LANES), jnp.int32),
             pltpu.VMEM((PACK, SUBLANES, held * LANES), jnp.int32),
             pltpu.VMEM((2, 16, held * LANES), jnp.bfloat16),
-            pltpu.VMEM((slots, 4, SUBLANES, LANES), jnp.float32),
+            pltpu.VMEM((2, slots, 4, SUBLANES, LANES), jnp.float32),
+            pltpu.VMEM((pairs,) + piece, jnp.float32),
             pltpu.VMEM((pairs,) + piece, jnp.float32),
             pltpu.VMEM((pairs,) + piece, jnp.float32),
             pltpu.VMEM((pairs - 1,) + piece, jnp.float32),
-            pltpu.VMEM((pairs - 1,) + piece, jnp.float32),
-            pltpu.VMEM(piece, jnp.float32),
             pltpu.VMEM((n, NODES, LANES), jnp.float32),
             pltpu.VMEM((m, NODES, LANES), jnp.float32),
             pltpu.SemaphoreType.DMA((2,)),
@@ -625,7 +622,7 @@
     def per_device(bins, grads, hess, node):
         features, rows = bins.shape
         own = features // n
-        if own == 32 and n % 2 == 0 and n > 2 and rows % (2 * SLOT) == 0:
+        if own == 32 and n % 2 == 0 and n > 2 and rows % (CHUNK * LANES) == 0:
             return grouped(n, m, bins, grads, hess, node)
         block = own if own < SUBLANES else next(b for b in (2 * SUBLANES, SUBLANES) if own % b == 0)
         held = max(block, SUBLANES)

time: 64.8 us -> 63.6 us (0.981)
  Pallas kernels: 61 us -> 59.8 us
    pallas_call x1, Pallas kernels: 12.9 us -> 11.9 us  [grouped(): pl.pallas_call(regroup, in_specs=[hbm, vmem, vmem, vmem], out_specs=(vmem...]
where the time goes in v3:
time: 63.6 us; the launch traced here: 63.3 us
  Pallas kernels  59.8 us (94%)
  other arithmetic  1.74 us (3%)
  local copies, waits for them, and re-layouts  1.09 us (2%)
  between operations  0.65 us (1%)
    pallas_call x1, Pallas kernels, grouped(): pl.pallas_call(functools.partial(sweep, n, m), in_specs=[hbm, vmem, vmem,...  48 us
    pallas_call x1, Pallas kernels, grouped(): pl.pallas_call(regroup, in_specs=[hbm, vmem, vmem, vmem], out_specs=(vmem...  11.9 us
    sub x1, other arithmetic, grouped(): return (out - best[None, :, None], best)  1.74 us

profile of v3, /device:TPU:0, one launch (start us, length us, event | category | flops | bytes accessed | tf_op | source)
XLA Modules:
  0.0 63.3 jit_solution(14727229496055654261)
XLA Ops:
  0.6 11.9 %shard_map.59 = (s32[79,8,8,128]{3,2,1,0:T(8,128)}, f32[79,8,128]{2,1,0:T(8,128)}, f32[40,128]{1,0:T(8,128)}, s32[1,128]{1,0:T(1,128)}) custom-call(s32[256,8192]{1,0:T(8,128)} %bins_hbm.1, s32[64,128]{1,0:T(8,128)} %bitcast.4, bf16[64,128]{1,0:T(8,128)(2,1)} %bitcast.5, bf16[64,128]{1,0:T(8,128)(2,1)} %bitcast.6), custom_call_target="tpu_custom_call" | custom-call | tf_op jit(solution)/shard_map/pallas_call | solution.py:559
  12.5 48.0 %shard_map.60 = (f32[32,8,256]{2,1,0:T(8,128)}, f32[1,8]{1,0:T(1,128)}) custom-call(s32[79,8,8,128]{3,2,1,0:T(8,128)} %get-tuple-element.8.words_hbm, f32[79,8,128]{2,1,0:T(8,128)} %get-tuple-element.9.gh_ref, f32[40,128]{1,0:T(8,128)} %get-tuple-element.10.keep_ref, s32[1,128]{1,0:T(1,128)} %get-tuple-element.11.last_ref), custom_call_target="tpu_custom_call" | custom-call | tf_op jit(solution)/shard_map/pallas_call | solution.py:582
  60.5 1.7 %broadcast_subtract_fusion = f32[32,8,256]{2,1,0:T(8,128)} fusion(f32[32,8,256]{2,1,0:T(8,128)} %get-tuple-element.12, f32[8]{0:T(128)} %bitcast.7), kind=kLoop, calls=%fused_computation | loop fusion | flops 65536 | bytes 524320 | tf_op jit(solution)/shard_map/sub | solution.py:616
  62.2 1.1 %copy.7 = f32[8]{0:T(128)} copy(f32[8]{0:T(128)} %bitcast.8) | data formatting | bytes 64

commit v4 on v3

--- a/solution.py
+++ b/solution.py
@@ -23,7 +23,6 @@
 PACK = 4
 CHUNK = 8
 DIGIT = 32
-BLOCKS = SUBLANES // 2
 
 
 def partner(me, k, n):
@@ -283,6 +282,9 @@
             for k in range(1, PACK):
                 word = word | lax.shift_left(bins[32 * t + SUBLANES * k : 32 * t + SUBLANES * (k + 1), cols], 8 * k)
             words.append(word)
+        for t in range(0, groups, 2):
+            one, two = words[t], words[t + 1]
+            words[t], words[t + 1] = jnp.where(sub < 4, one, two), jnp.where(sub < 4, two, one)
         piece = [jnp.broadcast_to(pieces[i, pl.ds(b, 1), :], (SUBLANES, LANES)) for i in range(2)]
         gh = jnp.where(sub == 0, piece[0], piece[1])
         for n in range(NODES):
@@ -319,40 +321,47 @@
     tiles = words.shape[1]
     slots = tiles * LANES // SLOT
     pairs = n // 2
+    order = [(0, 0), (0, 1)] + [(k, h) for h in range(2) for k in range(1, pairs - 1)] + [(pairs - 1, 0), (pairs - 1, 1)]
+    steps, away = 2 * pairs, 2 * (pairs - 1)
     me = lax.axis_index("row")
     mine = lax.axis_index("feat")
     chip, core = me // 2, me % 2
 
-    def to_chip(k):
-        return partner(chip, pairs - 1 - k, pairs)
-
-    def load(t):
-        group = 2 * to_chip(t // 2) + (t + 1 + core) % 2
-        return pltpu.make_async_copy(
-            words_hbm.at[pl.ds(0, tiles), group], words.at[t % 2], load_sem.at[t % 2]
-        )
-
-    def send_near(k, i):
+    def part(u, which):
+        value = order[0][which]
+        for i in range(1, steps):
+            value = jnp.where(u >= i, order[i][which], value)
+        return value
+
+    def to_chip(u):
+        return partner(chip, pairs - 1 - part(u, 0), pairs)
+
+    def load(u, e):
+        tile = 2 * to_chip(u) + part(u, 1)
+        return pltpu.make_async_copy(words_hbm.at[pl.ds(0, tiles), tile], words.at[e], load_sem.at[e])
+
+    def send_near(u):
         return pltpu.make_async_remote_copy(
-            src_ref=stage.at[k, i],
-            dst_ref=near.at[k, i],
-            send_sem=near_send.at[k, i],
-            recv_sem=near_recv.at[k, i],
+            src_ref=stage.at[u],
+            dst_ref=near.at[u],
+            send_sem=near_send.at[u],
+            recv_sem=near_recv.at[u],
             device_id={"row": 2 * chip + 1 - core},
             device_id_type=MESH,
         )
 
-    def send_far(k, i):
+    def send_far(u):
         return pltpu.make_async_remote_copy(
-            src_ref=relay.at[k, i],
-            dst_ref=far.at[k, i],
-            send_sem=far_send.at[k, i],
-            recv_sem=far_recv.at[k, i],
-            device_id={"row": 2 * to_chip(k) + core},
+            src_ref=relay.at[u],
+            dst_ref=far.at[u],
+            send_sem=far_send.at[u],
+            recv_sem=far_recv.at[u],
+            device_id={"row": 2 * to_chip(u) + core},
             device_id_type=MESH,
         )
 
-    load(0).start()
+    load(0, 0).start()
+    load(1, 1).start()
     barrier = pltpu.get_barrier_semaphore()
     for k in range(1, n):
         pl.semaphore_signal(barrier, inc=1, device_id={"row": (me + k) % n}, device_id_type=MESH)
@@ -373,20 +382,13 @@
     sub = lax.broadcasted_iota(jnp.int32, (SUBLANES, LANES), 0)
     byte = (lane // SUBLANES) % PACK
     of = [byte == f for f in range(PACK - 1)]
-    def unpack(t):
-        load(t).wait()
-
-        @pl.when(t + 1 < n)
-        def _():
-            load(t + 1).start()
-
-        for q in range(tiles):
-            word = words[t % 2, q]
-            for k in range(PACK):
-                keys[k, :, q * LANES : (q + 1) * LANES] = lax.shift_right_logical(word, 8 * k)
-
-    def one_hots(w, cols):
-        rows = [jnp.broadcast_to(keys[k, pl.ds(w, 1), cols], (SUBLANES, SLOT)) for k in range(PACK)]
+
+    def unpack(e, q):
+        for k in range(PACK):
+            keys[e, k, :, q * LANES : (q + 1) * LANES] = lax.shift_right_logical(words[e, q], 8 * k)
+
+    def one_hots(e, w, cols):
+        rows = [jnp.broadcast_to(keys[e, k, pl.ds(w, 1), cols], (SUBLANES, SLOT)) for k in range(PACK)]
         twos = [jnp.concatenate(rows[i : i + 2], 0).astype(jnp.int16) for i in (0, 2)]
         low = jnp.concatenate(rows, 0).astype(jnp.int8) & jnp.int8(DIGIT - 1)
         left = []
@@ -396,12 +398,12 @@
         right = [jnp.where(low != low_at[j], zero, one) for j in range(4)]
         return left, right
 
-    def block(i):
+    def block(e, w, side, hook):
         total = [jnp.zeros((SUBLANES, LANES), f32) for _ in range(4)]
         for s in range(slots):
             cols = slice(s * SLOT, (s + 1) * SLOT)
-            left0, right0 = one_hots(2 * i, cols)
-            left1, right1 = one_hots(2 * i + 1, cols)
+            left0, right0 = one_hots(e, w, cols)
+            left1, right1 = one_hots(e, w + 1, cols)
             found = lax.dot_general(
                 jnp.concatenate(left0 + left1, 0),
                 jnp.concatenate(right0 + right1, 0),
@@ -412,57 +414,81 @@
             for q in range(2):
                 square = found[64 * q : 64 * (q + 1), q * LANES : (q + 1) * LANES]
                 for v in range(2):
-                    part = [square[at : at + SUBLANES] for at in (16 * v, 16 * v + 8, 16 * v + 32, 16 * v + 40)]
-                    dense = jnp.where(of[0], part[0], jnp.where(of[1], part[1], jnp.where(of[2], part[2], part[3])))
+                    piece = [square[at : at + SUBLANES] for at in (16 * v, 16 * v + 8, 16 * v + 32, 16 * v + 40)]
+                    dense = jnp.where(of[0], piece[0], jnp.where(of[1], piece[1], jnp.where(of[2], piece[2], piece[3])))
                     at = 2 * q + v
                     total[at] = total[at] * kept + dense
-                    snap[i % 2, s, at] = total[at]
-
-    def store(ref, k, i):
+                    snap[side, s, at] = total[at]
+            hook(s)
+
+    def store(ref, u, b, side):
         for node in range(NODES):
             for at in range(4):
-                ref[k, i, node, at] = snap[i % 2, last_ref[0, node], at]
-
-    def merge(k, i):
-        send_near(k, i).wait_recv()
-        for node in range(NODES):
-            for at in range(4):
-                relay[k, i, node, at] += near[k, i, node, at]
-
-    def pair(k, carry):
-        unpack(2 * k)
-
-        @pl.when(k > 0)
+                ref[u, b, node, at] = snap[side, last_ref[0, node], at]
+
+    def merge(u):
+        for b in range(2):
+            for node in range(NODES):
+                for at in range(4):
+                    relay[u, b, node, at] += near[u, b, node, at]
+
+    middle = min(6, slots - 1)
+    load(0, 0).wait()
+    for q in range(tiles):
+        unpack(0, q)
+
+    def step(u, e):
+        @pl.when(u >= 2)
         def _():
-            for i in range(2, BLOCKS):
-                send_far(k - 1, i).start()
-
-        for i in range(BLOCKS):
-            block(i)
-            if i > 0:
-                send_near(k, i - 1).start()
-            store(stage, k, i)
-        unpack(2 * k + 1)
-        for i in range(BLOCKS):
-            if i == 0:
-                send_near(k, BLOCKS - 1).start()
-            if i == BLOCKS - 1:
-
-                @pl.when(k < pairs - 1)
-                def _():
-                    for j in range(2):
-                        send_far(k, j).start()
-
-            block(i)
-            store(relay, k, i)
-            if i == 1:
-                merge(k, 0)
-                merge(k, 1)
-        for i in range(2, BLOCKS):
-            merge(k, i)
+            send_near(u - 2).wait_recv()
+            merge(u - 2)
+
+        @pl.when(u >= 1)
+        def _():
+            send_near(u - 1).start()
+
+        @pl.when(u < steps - 1)
+        def _():
+            load(u + 1, 1 - e).wait()
+
+        @pl.when(u < steps - 2)
+        def _():
+            load(u + 2, e).start()
+
+        @pl.when((u >= 2) & (u - 2 < away))
+        def _():
+            send_far(u - 2).start()
+
+        half = part(u, 1)
+        give = 4 * ((1 - core + half) % 2)
+        hold = 4 * ((core + half) % 2)
+
+        def at_middle(*args):
+            def hook(s):
+                if s == middle:
+                    store(*args)
+
+            return hook
+
+        def third(s):
+            if s == middle:
+                store(stage, u, 1, 1)
+            for q in range(2 * s, 2 * s + 2):
+                unpack(1 - e, q)
+
+        block(e, give, 0, at_middle(relay, jnp.maximum(u - 1, 0), 1, 1))
+        block(e, give + 2, 1, at_middle(stage, u, 0, 0))
+        block(e, hold, 0, third)
+        block(e, hold + 2, 1, at_middle(relay, u, 0, 0))
+
+    def both(i, carry):
+        step(2 * i, 0)
+        step(2 * i + 1, 1)
         return carry
 
-    lax.fori_loop(0, pairs, pair, 0)
+    lax.fori_loop(0, pairs, both, 0)
+    send_near(steps - 1).start()
+    store(relay, steps - 1, 1, 1)
 
     tens, units = lane // (SUBLANES * PACK), lane % SUBLANES
     end_of_run = lane - units + (SUBLANES - 1)
@@ -480,42 +506,59 @@
             whole = whole + jnp.where(sub >= shift, pltpu.roll(whole, shift, 0), 0.0)
         return x + (whole - row), jnp.broadcast_to(whole[SUBLANES - 1 :], whole.shape)
 
-    def finish(i, best):
-        for k in range(pairs - 1):
-            send_far(k, i).wait_recv()
-        for q in range(2):
-            gains = []
+    def gains(h, best):
+        u = steps - 2 + h
+        sources = [v for v in range(away) if order[v][1] == h]
+        send_near(u).wait_recv()
+        for v in sources:
+            send_far(v).wait_recv()
+
+        def one_block(b, best):
+            tops = []
             for node in range(NODES):
-                sums = []
-                for at in (2 * q, 2 * q + 1):
-                    x = relay[pairs - 1, i, node, at]
-                    for k in range(pairs - 1):
-                        x = x + far[k, i, node, at]
-                    sums.append(running(x))
-                (gl, gt), (hl, ht) = sums
-                gain = gl * gl / (hl + 1.0)
-                gain = gain + (gt - gl) * (gt - gl) / (ht - hl + 1.0)
-                gains.append(gain - gt * gt / (ht + 1.0))
-            best = jnp.maximum(best, jnp.stack([jnp.max(x, axis=0) for x in gains], 0))
-            turned = jnp.swapaxes(jnp.stack(gains, 0), 0, 1)
-            for f in range(PACK):
-                source = ((lane // SUBLANES) % 4) * DIGIT + f * SUBLANES + units
-                for t in range(TOPS):
-                    part = [take(turned[4 * t + j], source) for j in range(4)]
-                    line = jnp.where(tens == 0, part[0], jnp.where(tens == 1, part[1], jnp.where(tens == 2, part[2], part[3])))
-                    out_ref[SUBLANES * f + 2 * i + q, :, t * LANES : (t + 1) * LANES] = line
-        return best
-
-    top_gain = lax.fori_loop(0, BLOCKS, finish, jnp.full((NODES, LANES), -jnp.inf, f32))
-
-    def exchange(value, slots, count, axis, index, sems, arrived):
-        slots[0] = jnp.broadcast_to(jnp.max(value, axis=1, keepdims=True), (NODES, LANES))
+                for q in range(2):
+                    sums = []
+                    for at in (2 * q, 2 * q + 1):
+                        x = relay[u, b, node, at] + near[u, b, node, at]
+                        for v in sources:
+                            x = x + far[v, b, node, at]
+                        sums.append(running(x))
+                    (gl, gt), (hl, ht) = sums
+                    gain = gl * gl / (hl + 1.0)
+                    gain = gain + (gt - gl) * (gt - gl) / (ht - hl + 1.0)
+                    gain = gain - gt * gt / (ht + 1.0)
+                    relay[u, b, node, 2 * q] = gain
+                    top = gain if q == 0 else jnp.maximum(top, gain)
+                tops.append(jnp.max(top, axis=0))
+            return jnp.maximum(best, jnp.stack(tops, 0))
+
+        return lax.fori_loop(0, 2, one_block, best)
+
+    def layout(h):
+        u = steps - 2 + h
+
+        def one_block(b, carry):
+            for q in range(2):
+                turned = jnp.swapaxes(jnp.stack([relay[u, b, node, 2 * q] for node in range(NODES)], 0), 0, 1)
+                for f in range(PACK):
+                    source = ((lane // SUBLANES) % 4) * DIGIT + f * SUBLANES + units
+                    for t in range(TOPS):
+                        piece = [take(turned[4 * t + j], source) for j in range(4)]
+                        line = jnp.where(tens == 0, piece[0], jnp.where(tens == 1, piece[1], jnp.where(tens == 2, piece[2], piece[3])))
+                        feature = SUBLANES * f + 4 * ((core + h) % 2) + 2 * b + q
+                        out_ref[feature, :, t * LANES : (t + 1) * LANES] = line
+            return carry
+
+        lax.fori_loop(0, 2, one_block, 0)
+
+    def exchange(value, parts, count, axis, index, sems, arrived, during):
+        parts[0] = jnp.broadcast_to(jnp.max(value, axis=1, keepdims=True), (NODES, LANES))
         copies = []
         for k in range(1, count):
             copies.append(
                 pltpu.make_async_remote_copy(
-                    src_ref=slots.at[0],
-                    dst_ref=slots.at[k],
+                    src_ref=parts.at[0],
+                    dst_ref=parts.at[k],
                     send_sem=sems.at[k - 1],
                     recv_sem=arrived.at[k - 1],
                     device_id={axis: (index + k) % count},
@@ -523,29 +566,27 @@
                 )
             )
             copies[-1].start()
+        during()
         for copy in copies:
             copy.wait()
-        best = slots[0]
+        best = parts[0]
         for k in range(1, count):
-            best = jnp.maximum(best, slots[k])
+            best = jnp.maximum(best, parts[k])
         return best
 
-    best = exchange(top_gain, row_best, n, "row", me, row_send, row_recv)
-    best = exchange(best, feat_best, m, "feat", mine, feat_send, feat_recv)
+    top_gain = jnp.full((NODES, LANES), -jnp.inf, f32)
+    send_near(steps - 2).wait_send()
+    for h in range(2):
+        top_gain = gains(h, top_gain)
+    best = exchange(top_gain, row_best, n, "row", me, row_send, row_recv, lambda: layout(0))
+    best = exchange(best, feat_best, m, "feat", mine, feat_send, feat_recv, lambda: layout(1))
     flat = jnp.max(jnp.where(lane == sub, best, -jnp.inf), axis=0, keepdims=True)
     best_ref[...] = flat[:, :NODES]
-
-    def drain(k, carry):
-        for i in range(BLOCKS):
-            send_near(k, i).wait_send()
-
-            @pl.when(k < pairs - 1)
-            def _():
-                send_far(k, i).wait_send()
-
-        return carry
-
-    lax.fori_loop(0, pairs, drain, 0)
+    for u in range(steps):
+        if u != steps - 2:
+            send_near(u).wait_send()
+        if u < away:
+            send_far(u).wait_send()
 
 
 def grouped(n, m, bins, grads, hess, node):
@@ -578,7 +619,8 @@
         compiler_params=pltpu.CompilerParams(vmem_limit_bytes=56 << 20),
     )(bins, node.reshape(-1, LANES), grads.reshape(-1, LANES), hess.reshape(-1, LANES))
     pairs = n // 2
-    piece = (BLOCKS, NODES, 4, SUBLANES, LANES)
+    piece = (2, NODES, 4, SUBLANES, LANES)
+    steps, away = 2 * pairs, 2 * (pairs - 1)
     out, best = pl.pallas_call(
         functools.partial(sweep, n, m),
         in_specs=[hbm, vmem, vmem, smem],
@@ -589,20 +631,20 @@
         ),
         scratch_shapes=[
             pltpu.VMEM((2, held, SUBLANES, LANES), jnp.int32),
-            pltpu.VMEM((PACK, SUBLANES, held * LANES), jnp.int32),
+            pltpu.VMEM((2, PACK, SUBLANES, held * LANES), jnp.int32),
             pltpu.VMEM((2, 16, held * LANES), jnp.bfloat16),
             pltpu.VMEM((2, slots, 4, SUBLANES, LANES), jnp.float32),
-            pltpu.VMEM((pairs,) + piece, jnp.float32),
-            pltpu.VMEM((pairs,) + piece, jnp.float32),
-            pltpu.VMEM((pairs,) + piece, jnp.float32),
-            pltpu.VMEM((pairs - 1,) + piece, jnp.float32),
+            pltpu.VMEM((steps,) + piece, jnp.float32),
+            pltpu.VMEM((steps,) + piece, jnp.float32),
+            pltpu.VMEM((steps,) + piece, jnp.float32),
+            pltpu.VMEM((away,) + piece, jnp.float32),
             pltpu.VMEM((n, NODES, LANES), jnp.float32),
             pltpu.VMEM((m, NODES, LANES), jnp.float32),
             pltpu.SemaphoreType.DMA((2,)),
-            pltpu.SemaphoreType.DMA((pairs, BLOCKS)),
-            pltpu.SemaphoreType.DMA((pairs, BLOCKS)),
-            pltpu.SemaphoreType.DMA((pairs - 1, BLOCKS)),
-            pltpu.SemaphoreType.DMA((pairs - 1, BLOCKS)),
+            pltpu.SemaphoreType.DMA((steps,)),
+            pltpu.SemaphoreType.DMA((steps,)),
+            pltpu.SemaphoreType.DMA((away,)),
+            pltpu.SemaphoreType.DMA((away,)),
             pltpu.SemaphoreType.DMA((n - 1,)),
             pltpu.SemaphoreType.DMA((n - 1,)),
             pltpu.SemaphoreType.DMA((m - 1,)),

time: 63.6 us -> 62.6 us (0.984)
  Pallas kernels: 59.8 us -> 58.8 us
    pallas_call x1, Pallas kernels: 48 us -> 47 us  [grouped(): pl.pallas_call(functools.partial(sweep, n, m), in_specs=[hbm, vmem, vmem,...]
where the time goes in v4:
time: 62.6 us; the launch traced here: 62.3 us
  Pallas kernels  58.8 us (94%)
  other arithmetic  1.74 us (3%)
  local copies, waits for them, and re-layouts  1.09 us (2%)
  between operations  0.65 us (1%)
    pallas_call x1, Pallas kernels, grouped(): pl.pallas_call(functools.partial(sweep, n, m), in_specs=[hbm, vmem, vmem,...  47 us
    pallas_call x1, Pallas kernels, grouped(): pl.pallas_call(regroup, in_specs=[hbm, vmem, vmem, vmem], out_specs=(vmem...  11.9 us
    sub x1, other arithmetic, grouped(): return (out - best[None, :, None], best)  1.74 us

profile of v4, /device:TPU:0, one launch (start us, length us, event | category | flops | bytes accessed | tf_op | source)
XLA Modules:
  0.0 62.3 jit_solution(12839905857073831875)
XLA Ops:
  0.6 11.9 %shard_map.59 = (s32[79,8,8,128]{3,2,1,0:T(8,128)}, f32[79,8,128]{2,1,0:T(8,128)}, f32[40,128]{1,0:T(8,128)}, s32[1,128]{1,0:T(1,128)}) custom-call(s32[256,8192]{1,0:T(8,128)} %bins_hbm.1, s32[64,128]{1,0:T(8,128)} %bitcast.4, bf16[64,128]{1,0:T(8,128)(2,1)} %bitcast.5, bf16[64,128]{1,0:T(8,128)(2,1)} %bitcast.6), custom_call_target="tpu_custom_call" | custom-call | tf_op jit(solution)/shard_map/pallas_call | solution.py:600
  12.5 47.0 %shard_map.60 = (f32[32,8,256]{2,1,0:T(8,128)}, f32[1,8]{1,0:T(1,128)}) custom-call(s32[79,8,8,128]{3,2,1,0:T(8,128)} %get-tuple-element.8.words_hbm, f32[79,8,128]{2,1,0:T(8,128)} %get-tuple-element.9.gh_ref, f32[40,128]{1,0:T(8,128)} %get-tuple-element.10.keep_ref, s32[1,128]{1,0:T(1,128)} %get-tuple-element.11.last_ref), custom_call_target="tpu_custom_call" | custom-call | tf_op jit(solution)/shard_map/pallas_call | solution.py:624
  59.5 1.7 %broadcast_subtract_fusion = f32[32,8,256]{2,1,0:T(8,128)} fusion(f32[32,8,256]{2,1,0:T(8,128)} %get-tuple-element.12, f32[8]{0:T(128)} %bitcast.7), kind=kLoop, calls=%fused_computation | loop fusion | flops 65536 | bytes 524320 | tf_op jit(solution)/shard_map/sub | solution.py:658
  61.2 1.1 %copy.7 = f32[8]{0:T(128)} copy(f32[8]{0:T(128)} %bitcast.8) | data formatting | bytes 64

commit v5 on v4

--- a/solution.py
+++ b/solution.py
@@ -321,23 +321,27 @@
     tiles = words.shape[1]
     slots = tiles * LANES // SLOT
     pairs = n // 2
-    order = [(0, 0), (0, 1)] + [(k, h) for h in range(2) for k in range(1, pairs - 1)] + [(pairs - 1, 0), (pairs - 1, 1)]
+    order = ((0, 0), (0, 1), (2, 0), (1, 1), (1, 0), (2, 1), (3, 0), (3, 1))
+    route = (2, 1, 2, 1, 1, 2, 3, 3)
     steps, away = 2 * pairs, 2 * (pairs - 1)
     me = lax.axis_index("row")
     mine = lax.axis_index("feat")
     chip, core = me // 2, me % 2
 
-    def part(u, which):
-        value = order[0][which]
+    def pick(u, table):
+        value = table[0]
         for i in range(1, steps):
-            value = jnp.where(u >= i, order[i][which], value)
+            value = jnp.where(u >= i, table[i], value)
         return value
 
-    def to_chip(u):
-        return partner(chip, pairs - 1 - part(u, 0), pairs)
+    def half_of(u):
+        return pick(u, [h for _, h in order])
+
+    def chip_at(k):
+        return partner(chip, pairs - 1 - k, pairs)
 
     def load(u, e):
-        tile = 2 * to_chip(u) + part(u, 1)
+        tile = 2 * chip_at(pick(u, [k for k, _ in order])) + half_of(u)
         return pltpu.make_async_copy(words_hbm.at[pl.ds(0, tiles), tile], words.at[e], load_sem.at[e])
 
     def send_near(u):
@@ -356,7 +360,7 @@
             dst_ref=far.at[u],
             send_sem=far_send.at[u],
             recv_sem=far_recv.at[u],
-            device_id={"row": 2 * to_chip(u) + core},
+            device_id={"row": 2 * chip_at(pick(u, route)) + core},
             device_id_type=MESH,
         )
 
@@ -426,11 +430,11 @@
             for at in range(4):
                 ref[u, b, node, at] = snap[side, last_ref[0, node], at]
 
-    def merge(u):
+    def merge(u, ref, v):
         for b in range(2):
             for node in range(NODES):
                 for at in range(4):
-                    relay[u, b, node, at] += near[u, b, node, at]
+                    relay[u, b, node, at] += ref[v, b, node, at]
 
     middle = min(6, slots - 1)
     load(0, 0).wait()
@@ -438,14 +442,19 @@
         unpack(0, q)
 
     def step(u, e):
+        @pl.when(u >= 1)
+        def _():
+            send_near(u - 1).start()
+
         @pl.when(u >= 2)
         def _():
             send_near(u - 2).wait_recv()
-            merge(u - 2)
-
-        @pl.when(u >= 1)
+            merge(u - 2, near, u - 2)
+
+        @pl.when(u >= away)
         def _():
-            send_near(u - 1).start()
+            send_far(u - away).wait_recv()
+            merge(u - 2, far, u - away)
 
         @pl.when(u < steps - 1)
         def _():
@@ -459,7 +468,7 @@
         def _():
             send_far(u - 2).start()
 
-        half = part(u, 1)
+        half = half_of(u)
         give = 4 * ((1 - core + half) % 2)
         hold = 4 * ((core + half) % 2)
 
@@ -508,7 +517,7 @@
 
     def gains(h, best):
         u = steps - 2 + h
-        sources = [v for v in range(away) if order[v][1] == h]
+        sources = [v for v in range(2, away) if order[v][1] == h]
         send_near(u).wait_recv()
         for v in sources:
             send_far(v).wait_recv()
@@ -664,7 +673,7 @@
     def per_device(bins, grads, hess, node):
         features, rows = bins.shape
         own = features // n
-        if own == 32 and n % 2 == 0 and n > 2 and rows % (CHUNK * LANES) == 0:
+        if own == 32 and n == 8 and rows % (CHUNK * LANES) == 0:
             return grouped(n, m, bins, grads, hess, node)
         block = own if own < SUBLANES else next(b for b in (2 * SUBLANES, SUBLANES) if own % b == 0)
         held = max(block, SUBLANES)

time: 62.6 us -> 60.8 us (0.971)
  Pallas kernels: 58.8 us -> 57.1 us
    pallas_call x1, Pallas kernels: 47 us -> 45.2 us  [grouped(): pl.pallas_call(functools.partial(sweep, n, m), in_specs=[hbm, vmem, vmem,...]
where the time goes in v5:
time: 60.8 us; the launch traced here: 60.5 us
  Pallas kernels  57.1 us (94%)
  other arithmetic  1.74 us (3%)
  local copies, waits for them, and re-layouts  1.09 us (2%)
  between operations  0.65 us (1%)
    pallas_call x1, Pallas kernels, grouped(): pl.pallas_call(functools.partial(sweep, n, m), in_specs=[hbm, vmem, vmem,...  45.2 us
    pallas_call x1, Pallas kernels, grouped(): pl.pallas_call(regroup, in_specs=[hbm, vmem, vmem, vmem], out_specs=(vmem...  11.9 us
    sub x1, other arithmetic, grouped(): return (out - best[None, :, None], best)  1.74 us

profile of v5, /device:TPU:0, one launch (start us, length us, event | category | flops | bytes accessed | tf_op | source)
XLA Modules:
  0.0 60.5 jit_solution(15290795642217254707)
XLA Ops:
  0.6 11.9 %shard_map.59 = (s32[79,8,8,128]{3,2,1,0:T(8,128)}, f32[79,8,128]{2,1,0:T(8,128)}, f32[40,128]{1,0:T(8,128)}, s32[1,128]{1,0:T(1,128)}) custom-call(s32[256,8192]{1,0:T(8,128)} %bins_hbm.1, s32[64,128]{1,0:T(8,128)} %bitcast.4, bf16[64,128]{1,0:T(8,128)(2,1)} %bitcast.5, bf16[64,128]{1,0:T(8,128)(2,1)} %bitcast.6), custom_call_target="tpu_custom_call" | custom-call | tf_op jit(solution)/shard_map/pallas_call | solution.py:609
  12.5 45.2 %shard_map.60 = (f32[32,8,256]{2,1,0:T(8,128)}, f32[1,8]{1,0:T(1,128)}) custom-call(s32[79,8,8,128]{3,2,1,0:T(8,128)} %get-tuple-element.8.words_hbm, f32[79,8,128]{2,1,0:T(8,128)} %get-tuple-element.9.gh_ref, f32[40,128]{1,0:T(8,128)} %get-tuple-element.10.keep_ref, s32[1,128]{1,0:T(1,128)} %get-tuple-element.11.last_ref), custom_call_target="tpu_custom_call" | custom-call | tf_op jit(solution)/shard_map/pallas_call | solution.py:633
  57.7 1.7 %broadcast_subtract_fusion = f32[32,8,256]{2,1,0:T(8,128)} fusion(f32[32,8,256]{2,1,0:T(8,128)} %get-tuple-element.12, f32[8]{0:T(128)} %bitcast.7), kind=kLoop, calls=%fused_computation | loop fusion | flops 65536 | bytes 524320 | tf_op jit(solution)/shard_map/sub | solution.py:667
  59.4 1.1 %copy.7 = f32[8]{0:T(128)} copy(f32[8]{0:T(128)} %bitcast.8) | data formatting | bytes 64

commit v6 on v5

--- a/solution.py
+++ b/solution.py
@@ -444,17 +444,14 @@
     def step(u, e):
         @pl.when(u >= 1)
         def _():
-            send_near(u - 1).start()
-
-        @pl.when(u >= 2)
+            store(relay, u - 1, 1, 1)
+            send_near(u - 1).wait_recv()
+            merge(u - 1, near, u - 1)
+
+        @pl.when((u >= away - 1) & (u < steps - 1))
         def _():
-            send_near(u - 2).wait_recv()
-            merge(u - 2, near, u - 2)
-
-        @pl.when(u >= away)
-        def _():
-            send_far(u - away).wait_recv()
-            merge(u - 2, far, u - away)
+            send_far(u - away + 1).wait_recv()
+            merge(u - 1, far, u - away + 1)
 
         @pl.when(u < steps - 1)
         def _():
@@ -464,9 +461,9 @@
         def _():
             load(u + 2, e).start()
 
-        @pl.when((u >= 2) & (u - 2 < away))
+        @pl.when((u >= 1) & (u <= away))
         def _():
-            send_far(u - 2).start()
+            send_far(u - 1).start()
 
         half = half_of(u)
         give = 4 * ((1 - core + half) % 2)
@@ -482,10 +479,12 @@
         def third(s):
             if s == middle:
                 store(stage, u, 1, 1)
+            if s == slots // 2:
+                send_near(u).start()
             for q in range(2 * s, 2 * s + 2):
                 unpack(1 - e, q)
 
-        block(e, give, 0, at_middle(relay, jnp.maximum(u - 1, 0), 1, 1))
+        block(e, give, 0, lambda s: None)
         block(e, give + 2, 1, at_middle(stage, u, 0, 0))
         block(e, hold, 0, third)
         block(e, hold + 2, 1, at_middle(relay, u, 0, 0))
@@ -496,8 +495,9 @@
         return carry
 
     lax.fori_loop(0, pairs, both, 0)
-    send_near(steps - 1).start()
     store(relay, steps - 1, 1, 1)
+    send_near(steps - 1).wait_recv()
+    merge(steps - 1, near, steps - 1)
 
     tens, units = lane // (SUBLANES * PACK), lane % SUBLANES
     end_of_run = lane - units + (SUBLANES - 1)
@@ -518,7 +518,6 @@
     def gains(h, best):
         u = steps - 2 + h
         sources = [v for v in range(2, away) if order[v][1] == h]
-        send_near(u).wait_recv()
         for v in sources:
             send_far(v).wait_recv()
 
@@ -528,7 +527,7 @@
                 for q in range(2):
                     sums = []
                     for at in (2 * q, 2 * q + 1):
-                        x = relay[u, b, node, at] + near[u, b, node, at]
+                        x = relay[u, b, node, at]
                         for v in sources:
                             x = x + far[v, b, node, at]
                         sums.append(running(x))
@@ -584,7 +583,6 @@
         return best
 
     top_gain = jnp.full((NODES, LANES), -jnp.inf, f32)
-    send_near(steps - 2).wait_send()
     for h in range(2):
         top_gain = gains(h, top_gain)
     best = exchange(top_gain, row_best, n, "row", me, row_send, row_recv, lambda: layout(0))
@@ -592,8 +590,7 @@
     flat = jnp.max(jnp.where(lane == sub, best, -jnp.inf), axis=0, keepdims=True)
     best_ref[...] = flat[:, :NODES]
     for u in range(steps):
-        if u != steps - 2:
-            send_near(u).wait_send()
+        send_near(u).wait_send()
         if u < away:
             send_far(u).wait_send()
 

time: 60.8 us -> 58.7 us (0.965)
  Pallas kernels: 57.1 us -> 54.9 us
    pallas_call x1, Pallas kernels: 45.2 us -> 43 us  [grouped(): pl.pallas_call(functools.partial(sweep, n, m), in_specs=[hbm, vmem, vmem,...]
where the time goes in v6:
time: 58.7 us; the launch traced here: 58.4 us
  Pallas kernels  54.9 us (94%)
  other arithmetic  1.74 us (3%)
  local copies, waits for them, and re-layouts  1.09 us (2%)
  between operations  0.65 us (1%)
    pallas_call x1, Pallas kernels, grouped(): pl.pallas_call(functools.partial(sweep, n, m), in_specs=[hbm, vmem, vmem,...  43 us
    pallas_call x1, Pallas kernels, grouped(): pl.pallas_call(regroup, in_specs=[hbm, vmem, vmem, vmem], out_specs=(vmem...  11.9 us
    sub x1, other arithmetic, grouped(): return (out - best[None, :, None], best)  1.74 us

profile of v6, /device:TPU:0, one launch (start us, length us, event | category | flops | bytes accessed | tf_op | source)
XLA Modules:
  0.0 58.4 jit_solution(253986100109195787)
XLA Ops:
  0.6 11.9 %shard_map.59 = (s32[79,8,8,128]{3,2,1,0:T(8,128)}, f32[79,8,128]{2,1,0:T(8,128)}, f32[40,128]{1,0:T(8,128)}, s32[1,128]{1,0:T(1,128)}) custom-call(s32[256,8192]{1,0:T(8,128)} %bins_hbm.1, s32[64,128]{1,0:T(8,128)} %bitcast.4, bf16[64,128]{1,0:T(8,128)(2,1)} %bitcast.5, bf16[64,128]{1,0:T(8,128)(2,1)} %bitcast.6), custom_call_target="tpu_custom_call" | custom-call | tf_op jit(solution)/shard_map/pallas_call | solution.py:606
  12.5 43.0 %shard_map.60 = (f32[32,8,256]{2,1,0:T(8,128)}, f32[1,8]{1,0:T(1,128)}) custom-call(s32[79,8,8,128]{3,2,1,0:T(8,128)} %get-tuple-element.8.words_hbm, f32[79,8,128]{2,1,0:T(8,128)} %get-tuple-element.9.gh_ref, f32[40,128]{1,0:T(8,128)} %get-tuple-element.10.keep_ref, s32[1,128]{1,0:T(1,128)} %get-tuple-element.11.last_ref), custom_call_target="tpu_custom_call" | custom-call | tf_op jit(solution)/shard_map/pallas_call | solution.py:630
  55.5 1.7 %broadcast_subtract_fusion = f32[32,8,256]{2,1,0:T(8,128)} fusion(f32[32,8,256]{2,1,0:T(8,128)} %get-tuple-element.12, f32[8]{0:T(128)} %bitcast.7), kind=kLoop, calls=%fused_computation | loop fusion | flops 65536 | bytes 524320 | tf_op jit(solution)/shard_map/sub | solution.py:664
  57.3 1.1 %copy.7 = f32[8]{0:T(128)} copy(f32[8]{0:T(128)} %bitcast.8) | data formatting | bytes 64

commit v7 on v6

--- a/solution.py
+++ b/solution.py
@@ -622,7 +622,7 @@
             pltpu.SemaphoreType.DMA((tiles // CHUNK,)),
             pltpu.SemaphoreType.DMA,
         ],
-        compiler_params=pltpu.CompilerParams(vmem_limit_bytes=56 << 20),
+        compiler_params=pltpu.CompilerParams(vmem_limit_bytes=50 << 20),
     )(bins, node.reshape(-1, LANES), grads.reshape(-1, LANES), hess.reshape(-1, LANES))
     pairs = n // 2
     piece = (2, NODES, 4, SUBLANES, LANES)
@@ -657,7 +657,7 @@
             pltpu.SemaphoreType.DMA((m - 1,)),
         ],
         compiler_params=pltpu.CompilerParams(
-            collective_id=0, has_side_effects=True, vmem_limit_bytes=56 << 20
+            collective_id=0, has_side_effects=True, vmem_limit_bytes=20 << 20
         ),
     )(words, gh, keep, last)
     best = best.reshape(NODES)

time: 58.7 us -> 56.8 us (0.968)
  Pallas kernels: 54.9 us -> 52.3 us
  local copies, waits for them, and re-layouts: 1.09 us -> 2.7 us
  other arithmetic: 1.74 us -> 0.79 us
    pallas_call x1, Pallas kernels: 11.9 us -> 10.2 us  [grouped(): pl.pallas_call(regroup, in_specs=[hbm, vmem, vmem, vmem], out_specs=(vmem...]
    unnamed x1 -> x7, local copies, waits for them, and re-layouts: 1.09 us -> 2.7 us
    sub x1, other arithmetic: 1.74 us -> 0.79 us  [grouped(): return (out - best[None, :, None], best)]
    pallas_call x1, Pallas kernels: 43 us -> 42.1 us  [grouped(): pl.pallas_call(functools.partial(sweep, n, m), in_specs=[hbm, vmem, vmem,...]
where the time goes in v7:
time: 56.8 us; the launch traced here: 56.5 us
  Pallas kernels  52.3 us (92%)
  local copies, waits for them, and re-layouts  2.7 us (5%)
  other arithmetic  0.79 us (1%)
  between operations  0.66 us (1%)
    pallas_call x1, Pallas kernels, grouped(): pl.pallas_call(functools.partial(sweep, n, m), in_specs=[hbm, vmem, vmem,...  42.1 us
    pallas_call x1, Pallas kernels, grouped(): pl.pallas_call(regroup, in_specs=[hbm, vmem, vmem, vmem], out_specs=(vmem...  10.2 us
    unnamed x7, local copies, waits for them, and re-layouts  2.7 us

profile of v7, /device:TPU:0, one launch (start us, length us, event | category | flops | bytes accessed | tf_op | source)
XLA Modules:
  0.0 56.5 jit_solution(8601026592140804855)
XLA Ops:
  0.6 0.0 copy-start
  0.6 0.7 %copy-done = s32[8192]{0:T(1024)S(1)} copy-done((s32[8192]{0:T(1024)S(1)}, s32[8192]{0:T(1024)}, u32[]{:S(2)}) %copy-start) | copy-done | bytes 32792
  1.4 0.0 copy-start.1
  1.4 0.7 %copy-done.1 = bf16[8192]{0:T(1024)(128)(2,1)S(1)} copy-done((bf16[8192]{0:T(1024)(128)(2,1)S(1)}, bf16[8192]{0:T(1024)(128)(2,1)}, u32[]{:S(2)}) %copy-start.1) | copy-done | bytes 16408
  2.1 0.0 copy-start.2
  2.1 0.7 %copy-done.2 = bf16[8192]{0:T(1024)(128)(2,1)S(1)} copy-done((bf16[8192]{0:T(1024)(128)(2,1)S(1)}, bf16[8192]{0:T(1024)(128)(2,1)}, u32[]{:S(2)}) %copy-start.2) | copy-done | bytes 16408
  2.8 10.2 %shard_map.59 = (s32[79,8,8,128]{3,2,1,0:T(8,128)S(1)}, f32[79,8,128]{2,1,0:T(8,128)S(1)}, f32[40,128]{1,0:T(8,128)S(1)}, s32[1,128]{1,0:T(1,128)S(1)}) custom-call(s32[256,8192]{1,0:T(8,128)} %bins_hbm.1, s32[64,128]{1,0:T(8,128)S(1)} %bitcast.4, bf16[64,128]{1,0:T(8,128)(2,1)S(1)} %bitcast.5, bf16[64,128]{1,0:T(8,128)(2,1)S(1)} %bitcast.6), custom_call_target="tpu_custom_call" | custom-call | tf_op jit(solution)/shard_map/pallas_call | solution.py:606
  13.1 42.1 %shard_map.60 = (f32[32,8,256]{2,1,0:T(8,128)S(1)}, f32[1,8]{1,0:T(1,128)S(1)}) custom-call(s32[79,8,8,128]{3,2,1,0:T(8,128)S(1)} %get-tuple-element.8.words_hbm, f32[79,8,128]{2,1,0:T(8,128)S(1)} %get-tuple-element.9.gh_ref, f32[40,128]{1,0:T(8,128)S(1)} %get-tuple-element.10.keep_ref, s32[1,128]{1,0:T(1,128)S(1)} %get-tuple-element.11.last_ref), custom_call_target="tpu_custom_call" | custom-call | tf_op jit(solution)/shard_map/pallas_call | solution.py:630
  55.2 0.8 %broadcast_subtract_fusion = f32[32,8,256]{2,1,0:T(8,128)} fusion(f32[32,8,256]{2,1,0:T(8,128)S(1)} %get-tuple-element.12, f32[8]{0:T(128)S(1)} %bitcast.7), kind=kLoop, calls=%fused_computation | loop fusion | flops 65536 | bytes 524320 | tf_op jit(solution)/shard_map/sub | solution.py:664
  56.0 0.5 copy.7
Async XLA Ops:
  0.6 0.8 %copy-start = (s32[8192]{0:T(1024)S(1)}, s32[8192]{0:T(1024)}, u32[]{:S(2)}) copy-start(s32[8192]{0:T(1024)} %param.7) | copy-start | bytes 98308
  1.4 0.7 %copy-start.1 = (bf16[8192]{0:T(1024)(128)(2,1)S(1)}, bf16[8192]{0:T(1024)(128)(2,1)}, u32[]{:S(2)}) copy-start(bf16[8192]{0:T(1024)(128)(2,1)} %param.5) | copy-start | bytes 49156
  2.1 0.7 %copy-start.2 = (bf16[8192]{0:T(1024)(128)(2,1)S(1)}, bf16[8192]{0:T(1024)(128)(2,1)}, u32[]{:S(2)}) copy-start(bf16[8192]{0:T(1024)(128)(2,1)} %param.6) | copy-start | bytes 49156

commit v8 on v7

--- a/solution.py
+++ b/solution.py
@@ -216,7 +216,7 @@
 
     for c in range(chunks):
         load(c).start()
-    node = node_ref[...]
+    node = node_ref[...].astype(i32)
     pieces[0] = g_ref[...].astype(f32)
     pieces[1] = h_ref[...].astype(f32)
     row = lax.broadcasted_iota(i32, (LANES, LANES), 0)
@@ -623,7 +623,7 @@
             pltpu.SemaphoreType.DMA,
         ],
         compiler_params=pltpu.CompilerParams(vmem_limit_bytes=50 << 20),
-    )(bins, node.reshape(-1, LANES), grads.reshape(-1, LANES), hess.reshape(-1, LANES))
+    )(bins, *(x.astype(jnp.float32).reshape(-1, LANES) for x in (node, grads, hess)))
     pairs = n // 2
     piece = (2, NODES, 4, SUBLANES, LANES)
     steps, away = 2 * pairs, 2 * (pairs - 1)

time: 56.8 us -> 56 us (0.986)
  local copies, waits for them, and re-layouts: 2.7 us -> 0.51 us
  other arithmetic: 0.79 us -> 2.29 us
    unnamed x7 -> x1, local copies, waits for them, and re-layouts: 2.7 us -> 0.51 us
    reshape x0 -> x2, other arithmetic: none -> 1.5 us  [grouped(): x.astype(jnp.float32).reshape(-1, LANES)]
where the time goes in v8:
time: 56 us; the launch traced here: 55.6 us
  Pallas kernels  52.2 us (93%)
  other arithmetic  2.29 us (4%)
  between operations  0.65 us (1%)
    pallas_call x1, Pallas kernels, grouped(): pl.pallas_call(functools.partial(sweep, n, m), in_specs=[hbm, vmem, vmem,...  42.1 us
    pallas_call x1, Pallas kernels, grouped(): pl.pallas_call(regroup, in_specs=[hbm, vmem, vmem, vmem], out_specs=(vmem...  10.1 us
    reshape x2, other arithmetic, grouped(): x.astype(jnp.float32).reshape(-1, LANES)  1.5 us

profile of v8, /device:TPU:0, one launch (start us, length us, event | category | flops | bytes accessed | tf_op | source)
XLA Modules:
  0.0 55.6 jit_solution(5353079543821566976)
XLA Ops:
  0.6 0.8 %convert_bitcast_fusion.node_ref = f32[64,128]{1,0:T(8,128)S(1)} fusion(s32[8192]{0:T(1024)} %param.7), kind=kLoop, calls=%fused_computation.1 | loop fusion | flops 8192 | bytes 65536 | tf_op jit(solution)/shard_map/reshape | solution.py:626
  1.4 0.7 %bitcast_convert_fusion = (f32[64,128]{1,0:T(8,128)S(1)}, f32[64,128]{1,0:T(8,128)S(1)}) fusion(bf16[8192]{0:T(1024)(128)(2,1)} %param.6, bf16[8192]{0:T(1024)(128)(2,1)} %param.5), kind=kLoop, calls=%fused_computation.2 | loop fusion | flops 16384 | bytes 98304 | tf_op jit(solution)/shard_map/reshape | solution.py:626
  2.1 10.1 %shard_map.59 = (s32[79,8,8,128]{3,2,1,0:T(8,128)S(1)}, f32[79,8,128]{2,1,0:T(8,128)S(1)}, f32[40,128]{1,0:T(8,128)S(1)}, s32[1,128]{1,0:T(1,128)S(1)}) custom-call(s32[256,8192]{1,0:T(8,128)} %bins_hbm.1, f32[64,128]{1,0:T(8,128)S(1)} %convert_bitcast_fusion.node_ref, f32[64,128]{1,0:T(8,128)S(1)} %get-tuple-element.15.g_ref, ...), custom_call_target="tpu_custom_call" | custom-call | tf_op jit(solution)/shard_map/pallas_call | solution.py:606
  12.2 42.1 %shard_map.60 = (f32[32,8,256]{2,1,0:T(8,128)S(1)}, f32[1,8]{1,0:T(1,128)S(1)}) custom-call(s32[79,8,8,128]{3,2,1,0:T(8,128)S(1)} %get-tuple-element.8.words_hbm, f32[79,8,128]{2,1,0:T(8,128)S(1)} %get-tuple-element.9.gh_ref, f32[40,128]{1,0:T(8,128)S(1)} %get-tuple-element.10.keep_ref, s32[1,128]{1,0:T(1,128)S(1)} %get-tuple-element.11.last_ref), custom_call_target="tpu_custom_call" | custom-call | tf_op jit(solution)/shard_map/pallas_call | solution.py:630
  54.3 0.8 %broadcast_subtract_fusion = f32[32,8,256]{2,1,0:T(8,128)} fusion(f32[32,8,256]{2,1,0:T(8,128)S(1)} %get-tuple-element.12, f32[8]{0:T(128)S(1)} %bitcast.9), kind=kLoop, calls=%fused_computation | loop fusion | flops 65536 | bytes 524320 | tf_op jit(solution)/shard_map/sub | solution.py:664
  55.1 0.5 copy.7
